TPU v7x, 256 devices: a whole 4x4x8 slice. The times are simulated.
256 devices in a mesh: section: 8 (over x, y_lo), dp: 32 (over y_hi, z, core).
Axes of the slice: x: 4, y: 4 (y_hi: 2, y_lo: 2; y = y_hi * 2 + y_lo), z: 8, core: 2. Of those that a mesh axis runs over, the one named last changes fastest.
Arguments:
- grid_latents: bfloat16 [96, 512, 512], P('dp'), may hold values from -6 to 6
- targets: bfloat16 [96, 512, 512], P('dp'), may hold values from -6 to 6
- g2m_tiles: bfloat16 [4, 128, 128], replicated, may hold values from -0.375 to 0.375
- g2m_cols: int32 [4], replicated, may hold values from 0 to 3
- m2m_tiles: bfloat16 [4, 128, 128], replicated, may hold values from -0.375 to 0.375
- m2m_cols: int32 [4], replicated, may hold values from 0 to 1
- m2g_tiles: bfloat16 [8, 128, 128], replicated, may hold values from -0.375 to 0.375
- m2g_cols: int32 [8], replicated, may hold values from 0 to 1
- w_msg: bfloat16 [8, 512, 512], P('section'), may hold values from -0.25 to 0.25
- w_up: bfloat16 [8, 512, 512], P('section'), may hold values from -0.25 to 0.25
- w_down: bfloat16 [8, 512, 512], P('section'), may hold values from -0.125 to 0.125
- gains: float32 [8, 512], P('section'), may hold values from 0.1 to 1.9
Outputs:
- weight_grads: float32 [8, 3, 512, 512], P('section')
- gain_grads: float32 [8, 512], P('section')
Inputs may be any that keep to these rules, and one draw needn't show every extreme that they name: `g2m_cols`: Grid-to-mesh tiles are listed by mesh row block in order, 2 to a block; tile t belongs to row block t // 2; column indices may repeat. `m2m_cols`: mesh tiles are listed by row block in order, 2 to a block; tile t belongs to row block t // 2. `m2g_cols`: Mesh-to-grid tiles are listed by grid row block in order, 2 to a block; tile t belongs to row block t // 2.
All inputs are finite; a program needn't handle non-finite values.
Results may differ from a plain program's by a relative error of at most 0.0034.
Values may be sent and summed in bfloat16 or wider, within the bound.
A program may use at most 64 MiB of HBM per device.

v0:
```python
import math

import jax
import jax.numpy as jnp
from jax import lax
from jax.sharding import PartitionSpec as P

NODES = 256
KG = 2
KM = 2
KD = 2


EPSILON = 1e-05


def shifted(block, axis, distance):
    devices = range(lax.axis_size(axis))
    route = [(i - distance, i) for i in devices if i - distance in devices]
    return lax.ppermute(block, axis, route)


def select_blocks(cols, source, tile_size):
    features = source.shape[1]
    blocks = source.reshape(-1, tile_size, features)
    picked = jnp.zeros((cols.shape[0], tile_size, features), source.dtype)
    for column in range(blocks.shape[0]):
        picked = jnp.where((cols == column)[:, None, None], blocks[column][None], picked)
    return picked


def block_apply(tiles, cols, source, fanout):
    tile_size = tiles.shape[-1]
    features = source.shape[1]
    picked = select_blocks(cols, source, tile_size)
    groups = tiles.shape[0] // fanout
    tiles_four = tiles.reshape(groups, fanout, tile_size, tile_size)
    picked_four = picked.reshape(groups, fanout, tile_size, features)
    summed = jnp.einsum(
        "rkij,rkjd->rid", tiles_four, picked_four, preferred_element_type=jnp.float32
    )
    return summed.reshape(groups * tile_size, features)


def block_transpose(tiles, cols, grad, fanout, blocks_out):
    tile_size = tiles.shape[-1]
    features = grad.shape[1]
    groups = tiles.shape[0] // fanout
    tiles_four = tiles.reshape(groups, fanout, tile_size, tile_size)
    grad_three = grad.reshape(groups, tile_size, features)
    products = jnp.einsum(
        "rkji,rjd->rkid", tiles_four, grad_three, preferred_element_type=jnp.float32
    )
    products = products.reshape(tiles.shape[0], tile_size, features)
    columns = [
        jnp.sum(jnp.where((cols == column)[:, None, None], products, 0.0), axis=0)
        for column in range(blocks_out)
    ]
    return jnp.stack(columns).reshape(blocks_out * tile_size, features)


def layer_forward(inputs, weights, tiles, cols):
    w_m, w_u, w_d, gain = weights
    center = inputs - jnp.mean(inputs, axis=-1, keepdims=True)
    inverse = lax.rsqrt(jnp.mean(center * center, axis=-1, keepdims=True) + EPSILON)
    normed = center * inverse
    unit = (normed * gain).astype(jnp.bfloat16)
    message = jnp.dot(unit, w_m, preferred_element_type=jnp.float32).astype(jnp.bfloat16)
    before = jnp.dot(unit, w_u, preferred_element_type=jnp.float32) + block_apply(
        tiles, cols, message, KM
    )
    active = jax.nn.silu(before).astype(jnp.bfloat16)
    output = inputs + jnp.dot(active, w_d, preferred_element_type=jnp.float32)
    return (output, (normed, inverse, unit, before, active))


def layer_backward(inputs, upstream, weights, tiles, cols, blocks_out):
    w_m, w_u, w_d, gain = weights
    unused, saved = layer_forward(inputs, weights, tiles, cols)
    normed, inverse, unit, before, active = saved
    over_rows = (((0,), (0,)), ((), ()))
    over_cols = (((1,), (1,)), ((), ()))
    grad_down = lax.dot_general(active, upstream, over_rows, preferred_element_type=jnp.float32)
    grad_active = lax.dot_general(upstream, w_d, over_cols, preferred_element_type=jnp.float32)
    sigma = jax.nn.sigmoid(before)
    grad_before = (grad_active * sigma * (1.0 + before * (1.0 - sigma))).astype(jnp.bfloat16)
    grad_up = lax.dot_general(unit, grad_before, over_rows, preferred_element_type=jnp.float32)
    grad_message = block_transpose(tiles, cols, grad_before, KM, blocks_out).astype(jnp.bfloat16)
    grad_msgw = lax.dot_general(unit, grad_message, over_rows, preferred_element_type=jnp.float32)
    grad_unit = lax.dot_general(
        grad_before, w_u, over_cols, preferred_element_type=jnp.float32
    ) + lax.dot_general(grad_message, w_m, over_cols, preferred_element_type=jnp.float32)
    grad_gain = jnp.sum(grad_unit * normed, axis=0)
    grad_normed = grad_unit * gain
    grad_inputs = upstream.astype(jnp.float32) + inverse * (
        grad_normed
        - jnp.mean(grad_normed, axis=-1, keepdims=True)
        - normed * jnp.mean(grad_normed * normed, axis=-1, keepdims=True)
    )
    return (grad_inputs, (grad_msgw, grad_up, grad_down, grad_gain))


def on_device(
    grid_latents,
    targets,
    g2m_tiles,
    g2m_cols,
    m2m_tiles,
    m2m_cols,
    m2g_tiles,
    m2g_cols,
    w_msg,
    w_up,
    w_down,
    gains,
):
    section_index = lax.axis_index("section")
    section_count = lax.axis_size("section")
    batch = grid_latents.shape[0]
    features = w_msg.shape[-1]
    local_layers = w_msg.shape[0]
    tile_size = m2m_tiles.shape[-1]
    mesh_blocks = NODES // tile_size
    layer_weights = [(w_msg[0], w_up[0], w_down[0], gains[0])]
    loss_scale = 1.0 / math.sqrt(batch * lax.axis_size("dp") * grid_latents.shape[1])
    is_first = section_index == 0
    is_last = section_index == section_count - 1
    zero_rows = jnp.zeros((NODES, features), jnp.bfloat16)
    empty_store = jnp.zeros((local_layers, batch, NODES, features), jnp.bfloat16)
    empty_seeds = jnp.zeros((batch, NODES, features), jnp.bfloat16)
    square = jnp.zeros((local_layers, features, features), jnp.float32)
    zero_totals = (square, square, square, jnp.zeros((local_layers, features), jnp.float32))

    def encode(index):
        grid_rows = lax.dynamic_index_in_dim(grid_latents, index, 0, keepdims=False)
        return block_apply(g2m_tiles, g2m_cols, grid_rows, KG).astype(jnp.bfloat16)

    def seed_of(rows_out, index):
        target = lax.dynamic_index_in_dim(targets, index, 0, keepdims=False)
        predicted = block_apply(m2g_tiles, m2g_cols, rows_out, KD)
        residual = ((predicted - target.astype(jnp.float32)) * loss_scale).astype(jnp.bfloat16)
        return block_transpose(m2g_tiles, m2g_cols, residual, KD, mesh_blocks).astype(jnp.bfloat16)

    def run_forward(received, index, stored, seeds):
        rows = lax.cond(is_first, lambda: encode(index), lambda: received)
        updated = lax.dynamic_update_index_in_dim(stored[0], rows, index, 0)
        stored = stored.at[0].set(updated)
        output, unused = layer_forward(
            rows.astype(jnp.float32), layer_weights[0], m2m_tiles, m2m_cols
        )
        rows = output.astype(jnp.bfloat16)
        seed = lax.cond(is_last, lambda: seed_of(rows, index), lambda: zero_rows)
        seeds = lax.dynamic_update_index_in_dim(seeds, seed, index, 0)
        return (rows, stored, seeds)

    def skip_forward(received, index, stored, seeds):
        return (zero_rows, stored, seeds)

    def run_backward(received, index, stored, seeds, totals):
        own_seed = lax.dynamic_index_in_dim(seeds, index, 0, keepdims=False)
        upstream = jnp.where(is_last, own_seed, received)
        grad_m, grad_u, grad_d, grad_g = totals
        for layer in reversed(range(local_layers)):
            rows_in = lax.dynamic_index_in_dim(stored[layer], index, 0, keepdims=False)
            grad_inputs, terms = layer_backward(
                rows_in.astype(jnp.float32),
                upstream,
                layer_weights[layer],
                m2m_tiles,
                m2m_cols,
                mesh_blocks,
            )
            upstream = grad_inputs.astype(jnp.bfloat16)
            grad_m = grad_m.at[layer].add(terms[0])
            grad_u = grad_u.at[layer].add(terms[1])
            grad_d = grad_d.at[layer].add(terms[2])
            grad_g = grad_g.at[layer].add(terms[3])
        return (upstream, (grad_m, grad_u, grad_d, grad_g))

    def skip_backward(received, index, stored, seeds, totals):
        return (zero_rows, totals)

    def forward_part(tick, received, stored, seeds):
        micro = tick - section_index
        live = (micro >= 0) & (micro < batch)
        index = jnp.clip(micro, 0, batch - 1)
        return lax.cond(live, run_forward, skip_forward, received, index, stored, seeds)

    def backward_part(tick, received, stored, seeds, totals, delay):
        micro = tick - (delay - section_index)
        live = (micro >= 0) & (micro < batch)
        index = jnp.clip(micro, 0, batch - 1)
        return lax.cond(live, run_backward, skip_backward, received, index, stored, seeds, totals)

    def forward_tick(tick, carry):
        received, stored, seeds = carry
        rows_out, stored, seeds = forward_part(tick, received, stored, seeds)
        received = shifted(rows_out, "section", 1)
        return (received, stored, seeds)

    unused_rows, stored, seeds = lax.fori_loop(
        0, batch + section_count - 1, forward_tick, (zero_rows, empty_store, empty_seeds)
    )

    def backward_tick(tick, carry):
        received, totals = carry
        grads_out, totals = backward_part(tick, received, stored, seeds, totals, section_count - 1)
        received = shifted(grads_out, "section", -1)
        return (received, totals)

    unused_grads, totals = lax.fori_loop(
        0, batch + section_count - 1, backward_tick, (zero_rows, zero_totals)
    )
    summed = lax.psum((totals[0], totals[1], totals[2], totals[3]), "dp")
    grad_weights = jnp.stack([summed[0], summed[1], summed[2]], axis=1)
    return (grad_weights, summed[3])


def solution(mesh):
    placed = (
        P("dp", None, None),
        P("dp", None, None),
        P(),
        P(),
        P(),
        P(),
        P(),
        P(),
        P("section", None, None),
        P("section", None, None),
        P("section", None, None),
        P("section", None),
    )
    return jax.shard_map(
        on_device,
        mesh=mesh,
        in_specs=placed,
        out_specs=(P("section", None, None, None), P("section", None)),
        check_vma=False,
    )
```

profile of v0, /device:TPU:1, one launch (start us, length us, event | category | flops | bytes accessed | tf_op | source)
XLA Modules:
  0.0 724.1 jit_solution(13097849197330674168)
XLA Ops:
  9.0 145.6 %while.49 = (s32[]{:T(128)}, bf16[256,512]{1,0:T(8,128)(2,1)}, bf16[1,3,256,512]{3,2,1,0:T(8,128)(2,1)S(1)}, bf16[3,256,512]{2,1,0:T(8,128)(2,1)}, s32[]{:T(128)...) while((s32[]{:T(128)}, bf16[256,512]{1,0:T(8,128)(2,1)}, ...), condition=%wide.region_12.13_spmd, body=%wide.region_0.12_spmd.sunk | while | flops 814350592 | bytes 19686080 | solution.py:201
  9.0 12.5 %conditional.7 = (bf16[256,512]{1,0:T(8,128)(2,1)}, bf16[1,3,256,512]{3,2,1,0:T(8,128)(2,1)S(1)}, bf16[3,256,512]{2,1,0:T(8,128)(2,1)}) conditional(s32[]{:T(128)} %convert_element_type.248, (bf16[1,3,256,512]{3,2,1,0:T(8,128)(2,1)S(1)}, bf16[3,256,512]{2,1,0:T(8,128)(2,1)}) %tuple.157, (pred[]{:T(512)}, s32[]{:T(128)}, bf16[256,512]{1,0:T(8,128)(2,1)}, ...), branch_computations={%region_1.1_spmd, %region_2.11_spmd} | conditional | flops 814350592 | bytes 18637070 | solution.py:187
  9.8 5.2 conditional.4
  26.4 12.5 %conditional.7 = (bf16[256,512]{1,0:T(8,128)(2,1)}, bf16[1,3,256,512]{3,2,1,0:T(8,128)(2,1)S(1)}, bf16[3,256,512]{2,1,0:T(8,128)(2,1)}) conditional(s32[]{:T(128)} %convert_element_type.248, (bf16[1,3,256,512]{3,2,1,0:T(8,128)(2,1)S(1)}, bf16[3,256,512]{2,1,0:T(8,128)(2,1)}) %tuple.157, (pred[]{:T(512)}, s32[]{:T(128)}, bf16[256,512]{1,0:T(8,128)(2,1)}, ...), branch_computations={%region_1.1_spmd, %region_2.11_spmd} | conditional | flops 814350592 | bytes 18637070 | solution.py:187
  27.3 5.2 conditional.4
  43.9 12.5 %conditional.7 = (bf16[256,512]{1,0:T(8,128)(2,1)}, bf16[1,3,256,512]{3,2,1,0:T(8,128)(2,1)S(1)}, bf16[3,256,512]{2,1,0:T(8,128)(2,1)}) conditional(s32[]{:T(128)} %convert_element_type.248, (bf16[1,3,256,512]{3,2,1,0:T(8,128)(2,1)S(1)}, bf16[3,256,512]{2,1,0:T(8,128)(2,1)}) %tuple.157, (pred[]{:T(512)}, s32[]{:T(128)}, bf16[256,512]{1,0:T(8,128)(2,1)}, ...), branch_computations={%region_1.1_spmd, %region_2.11_spmd} | conditional | flops 814350592 | bytes 18637070 | solution.py:187
  44.7 5.2 conditional.4
  62.0 13.2 %collective-permute-start = (bf16[256,512]{1,0:T(8,128)(2,1)}, bf16[256,512]{1,0:T(8,128)(2,1)}, u32[]{:S(2)}, u32[]{:S(2)}) collective-permute-start(bf16[256,512]{1,0:T(8,128)(2,1)} %get-tuple-element.1336), channel_id=1, source_target_pairs={{0,32},{32,64},{64,96},{96,128},{128,160},{160,192},{192,224},{1,3... | collective-permute-start | bytes 786440 | tf_op jit(solution)/shard_map/while/body/eval_jaxpr/ppermute | solution.py:20
  78.8 4.5 collective-permute-start
  87.4 12.4 %collective-permute-start = (bf16[256,512]{1,0:T(8,128)(2,1)}, bf16[256,512]{1,0:T(8,128)(2,1)}, u32[]{:S(2)}, u32[]{:S(2)}) collective-permute-start(bf16[256,512]{1,0:T(8,128)(2,1)} %get-tuple-element.1336), channel_id=1, source_target_pairs={{0,32},{32,64},{64,96},{96,128},{128,160},{160,192},{192,224},{1,3... | collective-permute-start | bytes 786440 | tf_op jit(solution)/shard_map/while/body/eval_jaxpr/ppermute | solution.py:20
  103.4 6.9 collective-permute-start
  110.4 5.2 collective-permute-done
  116.3 6.6 collective-permute-start
  128.0 7.0 collective-permute-start
  139.2 10.1 %collective-permute-start = (bf16[256,512]{1,0:T(8,128)(2,1)}, bf16[256,512]{1,0:T(8,128)(2,1)}, u32[]{:S(2)}, u32[]{:S(2)}) collective-permute-start(bf16[256,512]{1,0:T(8,128)(2,1)} %get-tuple-element.1336), channel_id=1, source_target_pairs={{0,32},{32,64},{64,96},{96,128},{128,160},{160,192},{192,224},{1,3... | collective-permute-start | bytes 786440 | tf_op jit(solution)/shard_map/while/body/eval_jaxpr/ppermute | solution.py:20
  149.3 5.3 collective-permute-done
  156.9 256.0 %while.50 = (s32[]{:T(128)}, bf16[256,512]{1,0:T(8,128)(2,1)S(1)}, f32[1,512,512]{2,1,0:T(8,128)}, f32[1,512,512]{2,1,0:T(8,128)S(1)}, f32[1,512,512]{2,1,0:T(8,...) while((s32[]{:T(128)}, bf16[256,512]{1,0:T(8,128)(2,1)S(1)}, ...), condition=%wide.region_23.24_spmd, body=%wide.region_13.23_spmd.sunk | while | flops 1218707712 | bytes 24952396 | solution.py:211
  159.0 7.3 %collective-permute-done.1 = bf16[256,512]{1,0:T(8,128)(2,1)S(1)} collective-permute-done((bf16[256,512]{1,0:T(8,128)(2,1)}, bf16[256,512]{1,0:T(8,128)(2,1)S(1)}, u32[]{:S(2)}, u32[]{:S(2)}) %collective-permute-start.1) | collective-permute-done | bytes 262176 | tf_op jit(solution)/shard_map/while/body/eval_jaxpr/ppermute | solution.py:20
  168.3 14.3 %collective-permute-done.1 = bf16[256,512]{1,0:T(8,128)(2,1)S(1)} collective-permute-done((bf16[256,512]{1,0:T(8,128)(2,1)}, bf16[256,512]{1,0:T(8,128)(2,1)S(1)}, u32[]{:S(2)}, u32[]{:S(2)}) %collective-permute-start.1) | collective-permute-done | bytes 262176 | tf_op jit(solution)/shard_map/while/body/eval_jaxpr/ppermute | solution.py:20
  184.6 10.1 %collective-permute-done.1 = bf16[256,512]{1,0:T(8,128)(2,1)S(1)} collective-permute-done((bf16[256,512]{1,0:T(8,128)(2,1)}, bf16[256,512]{1,0:T(8,128)(2,1)S(1)}, u32[]{:S(2)}, u32[]{:S(2)}) %collective-permute-start.1) | collective-permute-done | bytes 262176 | tf_op jit(solution)/shard_map/while/body/eval_jaxpr/ppermute | solution.py:20
  196.7 11.4 %collective-permute-done.1 = bf16[256,512]{1,0:T(8,128)(2,1)S(1)} collective-permute-done((bf16[256,512]{1,0:T(8,128)(2,1)}, bf16[256,512]{1,0:T(8,128)(2,1)S(1)}, u32[]{:S(2)}, u32[]{:S(2)}) %collective-permute-start.1) | collective-permute-done | bytes 262176 | tf_op jit(solution)/shard_map/while/body/eval_jaxpr/ppermute | solution.py:20
  210.2 10.3 %collective-permute-done.1 = bf16[256,512]{1,0:T(8,128)(2,1)S(1)} collective-permute-done((bf16[256,512]{1,0:T(8,128)(2,1)}, bf16[256,512]{1,0:T(8,128)(2,1)S(1)}, u32[]{:S(2)}, u32[]{:S(2)}) %collective-permute-start.1) | collective-permute-done | bytes 262176 | tf_op jit(solution)/shard_map/while/body/eval_jaxpr/ppermute | solution.py:20
  222.5 14.6 %collective-permute-done.1 = bf16[256,512]{1,0:T(8,128)(2,1)S(1)} collective-permute-done((bf16[256,512]{1,0:T(8,128)(2,1)}, bf16[256,512]{1,0:T(8,128)(2,1)S(1)}, u32[]{:S(2)}, u32[]{:S(2)}) %collective-permute-start.1) | collective-permute-done | bytes 262176 | tf_op jit(solution)/shard_map/while/body/eval_jaxpr/ppermute | solution.py:20
  239.2 103.5 %collective-permute-done.1 = bf16[256,512]{1,0:T(8,128)(2,1)S(1)} collective-permute-done((bf16[256,512]{1,0:T(8,128)(2,1)}, bf16[256,512]{1,0:T(8,128)(2,1)S(1)}, u32[]{:S(2)}, u32[]{:S(2)}) %collective-permute-start.1) | collective-permute-done | bytes 262176 | tf_op jit(solution)/shard_map/while/body/eval_jaxpr/ppermute | solution.py:20
  342.7 15.2 %conditional.8 = (bf16[256,512]{1,0:T(8,128)(2,1)}, f32[1,512,512]{2,1,0:T(8,128)}, f32[1,512,512]{2,1,0:T(8,128)S(1)}, f32[1,512,512]{2,1,0:T(8,128)}, f32[1,512]{1,0:T(1,128)S(1)}) conditional(s32[]{:T(128)} %convert_element_type.249, (f32[1,512,512]{2,1,0:T(8,128)}, f32[1,512,512]{2,1,0:T(8,128)S(1)}, f32[1,512,512]{2,1,0:T(8,128)}, ...), branch_computations={%region_14.14_spmd, %region_15.22_spmd} | conditional | flops 1218707712 | bytes 23903416 | solution.py:193
  359.2 6.9 collective-permute-done.1
  366.2 15.2 %conditional.8 = (bf16[256,512]{1,0:T(8,128)(2,1)}, f32[1,512,512]{2,1,0:T(8,128)}, f32[1,512,512]{2,1,0:T(8,128)S(1)}, f32[1,512,512]{2,1,0:T(8,128)}, f32[1,512]{1,0:T(1,128)S(1)}) conditional(s32[]{:T(128)} %convert_element_type.249, (f32[1,512,512]{2,1,0:T(8,128)}, f32[1,512,512]{2,1,0:T(8,128)S(1)}, f32[1,512,512]{2,1,0:T(8,128)}, ...), branch_computations={%region_14.14_spmd, %region_15.22_spmd} | conditional | flops 1218707712 | bytes 23903416 | solution.py:193
  382.7 6.9 collective-permute-done.1
  389.6 15.2 %conditional.8 = (bf16[256,512]{1,0:T(8,128)(2,1)}, f32[1,512,512]{2,1,0:T(8,128)}, f32[1,512,512]{2,1,0:T(8,128)S(1)}, f32[1,512,512]{2,1,0:T(8,128)}, f32[1,512]{1,0:T(1,128)S(1)}) conditional(s32[]{:T(128)} %convert_element_type.249, (f32[1,512,512]{2,1,0:T(8,128)}, f32[1,512,512]{2,1,0:T(8,128)S(1)}, f32[1,512,512]{2,1,0:T(8,128)}, ...), branch_computations={%region_14.14_spmd, %region_15.22_spmd} | conditional | flops 1218707712 | bytes 23903416 | solution.py:193
  406.2 6.8 collective-permute-done.1
  413.9 92.3 %psum.31 = f32[1,512]{1,0:T(1,128)} all-reduce(f32[1,512]{1,0:T(1,128)S(1)} %get-tuple-element.1012), channel_id=1, replica_groups=mesh['section'=8,'dp'=32] {'dp'}, use_global_device_ids=true, to_apply=%region_27.28 | all-reduce | flops 512 | bytes 4096 | tf_op jit(solution)/shard_map/psum | solution.py:214
  506.3 207.2 %all-reduce.3.cloned.1.call-done = (f32[1,1,512,512]{3,2,1,0:T(8,128)}, f32[1,1,512,512]{3,2,1,0:T(8,128)}, f32[1,1,512,512]{3,2,1,0:T(8,128)}) async-done(((f32[1,1,512,512]{3,2,1,0:T(8,128)}, f32[1,1,512,512]{3,2,1,0:T(8,128)}, f32[1,1,512,512]{3,2,1,0:T(8,128)}), (f32[1,1,512,512]{3,2,1,0:T(8,128)}, f32[1,1,512,512]{3,2,1,0:T(8,128)}, f32[1,1,512,512]{3,2,1,0:T(8,128)})) %all-reduce.3.cloned.1.call-update) | async-done | bytes 3145744 | tf_op jit(solution)/shard_map/psum | solution.py:214
  (242 shorter events, 156.4 us)
Async XLA Ops:
  7.2 706.3 %all-reduce.3.cloned.1.call-start = ((), (), s32[]{:S(2)}) async-start(), calls=%async_computation | async-start | bytes 6291456 | tf_op jit(solution)/shard_map/psum | solution.py:214
  9.8 6.4 copy-start.4
  9.8 7.9 %copy-start.7 = (bf16[4,128,128]{2,1,0:T(8,128)(2,1)S(1)}, bf16[4,128,128]{2,1,0:T(8,128)(2,1)}, u32[]{:S(2)}) copy-start(bf16[4,128,128]{2,1,0:T(8,128)(2,1)} %get-tuple-element.926) | copy-start | bytes 393220 | tf_op jit(solution)/shard_map/while/body/eval_jaxpr/cond
  15.0 3.1 copy-start
  18.1 2.6 copy-start.6
  21.5 4.9 collective-permute-start
  27.3 6.4 copy-start.4
  27.3 7.9 %copy-start.7 = (bf16[4,128,128]{2,1,0:T(8,128)(2,1)S(1)}, bf16[4,128,128]{2,1,0:T(8,128)(2,1)}, u32[]{:S(2)}) copy-start(bf16[4,128,128]{2,1,0:T(8,128)(2,1)} %get-tuple-element.926) | copy-start | bytes 393220 | tf_op jit(solution)/shard_map/while/body/eval_jaxpr/cond
  32.4 3.1 copy-start
  35.6 2.6 copy-start.6
  38.9 4.9 collective-permute-start
  44.7 6.4 copy-start.4
  44.7 7.9 %copy-start.7 = (bf16[4,128,128]{2,1,0:T(8,128)(2,1)S(1)}, bf16[4,128,128]{2,1,0:T(8,128)(2,1)}, u32[]{:S(2)}) copy-start(bf16[4,128,128]{2,1,0:T(8,128)(2,1)} %get-tuple-element.926) | copy-start | bytes 393220 | tf_op jit(solution)/shard_map/while/body/eval_jaxpr/cond
  49.9 3.1 copy-start
  56.4 4.9 collective-permute-start
  62.0 16.1 %collective-permute-start = (bf16[256,512]{1,0:T(8,128)(2,1)}, bf16[256,512]{1,0:T(8,128)(2,1)}, u32[]{:S(2)}, u32[]{:S(2)}) collective-permute-start(bf16[256,512]{1,0:T(8,128)(2,1)} %get-tuple-element.1336), channel_id=1, source_target_pairs={{0,32},{32,64},{64,96},{96,128},{128,160},{160,192},{192,224},{1,3... | collective-permute-start | bytes 786440 | tf_op jit(solution)/shard_map/while/body/eval_jaxpr/ppermute | solution.py:20
  78.8 7.8 %collective-permute-start = (bf16[256,512]{1,0:T(8,128)(2,1)}, bf16[256,512]{1,0:T(8,128)(2,1)}, u32[]{:S(2)}, u32[]{:S(2)}) collective-permute-start(bf16[256,512]{1,0:T(8,128)(2,1)} %get-tuple-element.1336), channel_id=1, source_target_pairs={{0,32},{32,64},{64,96},{96,128},{128,160},{160,192},{192,224},{1,3... | collective-permute-start | bytes 786440 | tf_op jit(solution)/shard_map/while/body/eval_jaxpr/ppermute | solution.py:20
  87.4 15.3 %collective-permute-start = (bf16[256,512]{1,0:T(8,128)(2,1)}, bf16[256,512]{1,0:T(8,128)(2,1)}, u32[]{:S(2)}, u32[]{:S(2)}) collective-permute-start(bf16[256,512]{1,0:T(8,128)(2,1)} %get-tuple-element.1336), channel_id=1, source_target_pairs={{0,32},{32,64},{64,96},{96,128},{128,160},{160,192},{192,224},{1,3... | collective-permute-start | bytes 786440 | tf_op jit(solution)/shard_map/while/body/eval_jaxpr/ppermute | solution.py:20
  103.4 12.2 %collective-permute-start = (bf16[256,512]{1,0:T(8,128)(2,1)}, bf16[256,512]{1,0:T(8,128)(2,1)}, u32[]{:S(2)}, u32[]{:S(2)}) collective-permute-start(bf16[256,512]{1,0:T(8,128)(2,1)} %get-tuple-element.1336), channel_id=1, source_target_pairs={{0,32},{32,64},{64,96},{96,128},{128,160},{160,192},{192,224},{1,3... | collective-permute-start | bytes 786440 | tf_op jit(solution)/shard_map/while/body/eval_jaxpr/ppermute | solution.py:20
  116.3 11.0 %collective-permute-start = (bf16[256,512]{1,0:T(8,128)(2,1)}, bf16[256,512]{1,0:T(8,128)(2,1)}, u32[]{:S(2)}, u32[]{:S(2)}) collective-permute-start(bf16[256,512]{1,0:T(8,128)(2,1)} %get-tuple-element.1336), channel_id=1, source_target_pairs={{0,32},{32,64},{64,96},{96,128},{128,160},{160,192},{192,224},{1,3... | collective-permute-start | bytes 786440 | tf_op jit(solution)/shard_map/while/body/eval_jaxpr/ppermute | solution.py:20
  128.0 10.5 %collective-permute-start = (bf16[256,512]{1,0:T(8,128)(2,1)}, bf16[256,512]{1,0:T(8,128)(2,1)}, u32[]{:S(2)}, u32[]{:S(2)}) collective-permute-start(bf16[256,512]{1,0:T(8,128)(2,1)} %get-tuple-element.1336), channel_id=1, source_target_pairs={{0,32},{32,64},{64,96},{96,128},{128,160},{160,192},{192,224},{1,3... | collective-permute-start | bytes 786440 | tf_op jit(solution)/shard_map/while/body/eval_jaxpr/ppermute | solution.py:20
  139.2 15.3 %collective-permute-start = (bf16[256,512]{1,0:T(8,128)(2,1)}, bf16[256,512]{1,0:T(8,128)(2,1)}, u32[]{:S(2)}, u32[]{:S(2)}) collective-permute-start(bf16[256,512]{1,0:T(8,128)(2,1)} %get-tuple-element.1336), channel_id=1, source_target_pairs={{0,32},{32,64},{64,96},{96,128},{128,160},{160,192},{192,224},{1,3... | collective-permute-start | bytes 786440 | tf_op jit(solution)/shard_map/while/body/eval_jaxpr/ppermute | solution.py:20
  157.7 8.6 %collective-permute-start.1 = (bf16[256,512]{1,0:T(8,128)(2,1)}, bf16[256,512]{1,0:T(8,128)(2,1)S(1)}, u32[]{:S(2)}, u32[]{:S(2)}) collective-permute-start(bf16[256,512]{1,0:T(8,128)(2,1)} %get-tuple-element.1355), channel_id=1, source_target_pairs={{32,0},{64,32},{96,64},{128,96},{160,128},{192,160},{224,192},{33,... | collective-permute-start | bytes 786440 | tf_op jit(solution)/shard_map/while/body/eval_jaxpr/ppermute | solution.py:20
  167.0 15.6 %collective-permute-start.1 = (bf16[256,512]{1,0:T(8,128)(2,1)}, bf16[256,512]{1,0:T(8,128)(2,1)S(1)}, u32[]{:S(2)}, u32[]{:S(2)}) collective-permute-start(bf16[256,512]{1,0:T(8,128)(2,1)} %get-tuple-element.1355), channel_id=1, source_target_pairs={{32,0},{64,32},{96,64},{128,96},{160,128},{192,160},{224,192},{33,... | collective-permute-start | bytes 786440 | tf_op jit(solution)/shard_map/while/body/eval_jaxpr/ppermute | solution.py:20
  183.3 11.4 %collective-permute-start.1 = (bf16[256,512]{1,0:T(8,128)(2,1)}, bf16[256,512]{1,0:T(8,128)(2,1)S(1)}, u32[]{:S(2)}, u32[]{:S(2)}) collective-permute-start(bf16[256,512]{1,0:T(8,128)(2,1)} %get-tuple-element.1355), channel_id=1, source_target_pairs={{32,0},{64,32},{96,64},{128,96},{160,128},{192,160},{224,192},{33,... | collective-permute-start | bytes 786440 | tf_op jit(solution)/shard_map/while/body/eval_jaxpr/ppermute | solution.py:20
  195.4 12.7 %collective-permute-start.1 = (bf16[256,512]{1,0:T(8,128)(2,1)}, bf16[256,512]{1,0:T(8,128)(2,1)S(1)}, u32[]{:S(2)}, u32[]{:S(2)}) collective-permute-start(bf16[256,512]{1,0:T(8,128)(2,1)} %get-tuple-element.1355), channel_id=1, source_target_pairs={{32,0},{64,32},{96,64},{128,96},{160,128},{192,160},{224,192},{33,... | collective-permute-start | bytes 786440 | tf_op jit(solution)/shard_map/while/body/eval_jaxpr/ppermute | solution.py:20
  208.9 11.6 %collective-permute-start.1 = (bf16[256,512]{1,0:T(8,128)(2,1)}, bf16[256,512]{1,0:T(8,128)(2,1)S(1)}, u32[]{:S(2)}, u32[]{:S(2)}) collective-permute-start(bf16[256,512]{1,0:T(8,128)(2,1)} %get-tuple-element.1355), channel_id=1, source_target_pairs={{32,0},{64,32},{96,64},{128,96},{160,128},{192,160},{224,192},{33,... | collective-permute-start | bytes 786440 | tf_op jit(solution)/shard_map/while/body/eval_jaxpr/ppermute | solution.py:20
  221.3 15.9 %collective-permute-start.1 = (bf16[256,512]{1,0:T(8,128)(2,1)}, bf16[256,512]{1,0:T(8,128)(2,1)S(1)}, u32[]{:S(2)}, u32[]{:S(2)}) collective-permute-start(bf16[256,512]{1,0:T(8,128)(2,1)} %get-tuple-element.1355), channel_id=1, source_target_pairs={{32,0},{64,32},{96,64},{128,96},{160,128},{192,160},{224,192},{33,... | collective-permute-start | bytes 786440 | tf_op jit(solution)/shard_map/while/body/eval_jaxpr/ppermute | solution.py:20
  237.9 104.8 %collective-permute-start.1 = (bf16[256,512]{1,0:T(8,128)(2,1)}, bf16[256,512]{1,0:T(8,128)(2,1)S(1)}, u32[]{:S(2)}, u32[]{:S(2)}) collective-permute-start(bf16[256,512]{1,0:T(8,128)(2,1)} %get-tuple-element.1355), channel_id=1, source_target_pairs={{32,0},{64,32},{96,64},{128,96},{160,128},{192,160},{224,192},{33,... | collective-permute-start | bytes 786440 | tf_op jit(solution)/shard_map/while/body/eval_jaxpr/ppermute | solution.py:20
  357.9 8.2 %collective-permute-start.1 = (bf16[256,512]{1,0:T(8,128)(2,1)}, bf16[256,512]{1,0:T(8,128)(2,1)S(1)}, u32[]{:S(2)}, u32[]{:S(2)}) collective-permute-start(bf16[256,512]{1,0:T(8,128)(2,1)} %get-tuple-element.1355), channel_id=1, source_target_pairs={{32,0},{64,32},{96,64},{128,96},{160,128},{192,160},{224,192},{33,... | collective-permute-start | bytes 786440 | tf_op jit(solution)/shard_map/while/body/eval_jaxpr/ppermute | solution.py:20
  381.4 8.2 %collective-permute-start.1 = (bf16[256,512]{1,0:T(8,128)(2,1)}, bf16[256,512]{1,0:T(8,128)(2,1)S(1)}, u32[]{:S(2)}, u32[]{:S(2)}) collective-permute-start(bf16[256,512]{1,0:T(8,128)(2,1)} %get-tuple-element.1355), channel_id=1, source_target_pairs={{32,0},{64,32},{96,64},{128,96},{160,128},{192,160},{224,192},{33,... | collective-permute-start | bytes 786440 | tf_op jit(solution)/shard_map/while/body/eval_jaxpr/ppermute | solution.py:20
  404.9 8.1 %collective-permute-start.1 = (bf16[256,512]{1,0:T(8,128)(2,1)}, bf16[256,512]{1,0:T(8,128)(2,1)S(1)}, u32[]{:S(2)}, u32[]{:S(2)}) collective-permute-start(bf16[256,512]{1,0:T(8,128)(2,1)} %get-tuple-element.1355), channel_id=1, source_target_pairs={{32,0},{64,32},{96,64},{128,96},{160,128},{192,160},{224,192},{33,... | collective-permute-start | bytes 786440 | tf_op jit(solution)/shard_map/while/body/eval_jaxpr/ppermute | solution.py:20
  (11 other events, 24.5 us)
Sparse Core Ops, SparseCore 0:
  414.1 299.3 all-reduce.2
where the time goes:
time: 726 us; the launch traced here: 724 us
  waiting for transfers between devices  436 us (60%)
  blocking collectives  92.3 us (13%)
  starting transfers between devices  79.6 us (11%)
  matrix products  54.6 us (8%)
  local copies, waits for them, and re-layouts  26.4 us (4%)
  other arithmetic  20.6 us (3%)
  between operations  14.1 us (2%)
    ppermute x20, waiting for transfers between devices, shifted(): return lax.ppermute(block, axis, route)  228 us
    psum x1, waiting for transfers between devices, on_device(): summed = lax.psum((totals[0], totals[1], totals[2], totals[3]), 'dp')  207 us
    psum x1, blocking collectives, on_device(): summed = lax.psum((totals[0], totals[1], totals[2], totals[3]), 'dp')  92.3 us
    ppermute x20, starting transfers between devices, shifted(): return lax.ppermute(block, axis, route)  79.5 us
  transfers between devices with their start and end apart: 21, of which 21 were waited for; matrix products, arithmetic and copies ran while one was open for 0% of the time, Pallas kernels for 0%

commit v1 on v0

v1 whole, which is shorter than its diff:
```python
import functools
import math

import jax
import jax.numpy as jnp
from jax import lax
from jax.experimental import pallas as pl
from jax.experimental.pallas import tpu as pltpu
from jax.sharding import PartitionSpec as P

BLOCK = 128
NODES = 256
EPSILON = 1e-05
MESH = pl.DeviceIdType.MESH
F32 = jnp.float32
BF16 = jnp.bfloat16
CHUNKS = 2
CORES = 2
RING = 8
STEPS = RING - 1
SUBS = 2


def dot(a, b):
    return jnp.dot(a, b, preferred_element_type=F32)


def dot_nt(a, b):
    return lax.dot_general(a, b, (((1,), (1,)), ((), ())), preferred_element_type=F32)


def step_kernel(
    sections,
    halves,
    samples,
    loss_scale,
    lat_hbm,
    tgt_hbm,
    g2m_hbm,
    g2m_c,
    m2m_hbm,
    m2m_c,
    m2g_hbm,
    m2g_c,
    wm_hbm,
    wu_hbm,
    wd_hbm,
    gain_hbm,
    out,
    gain_out,
    lat,
    tgt,
    g2m,
    m2m,
    m2g,
    wm,
    wu,
    wd,
    gain_v,
    mix,
    mix_t,
    enc,
    pred,
    seed_t,
    xin,
    xout,
    gin,
    gout,
    unit_s,
    unit_t,
    act_t,
    slope_s,
    normed_s,
    inv_s,
    msg_s,
    up_s,
    gb_s,
    gm_s,
    acc,
    gacc,
    sib_buf,
    ring_buf,
    y_buf,
    g_sib,
    g_y,
    g_z,
    in_sem,
    lat_sem,
    tgt_sem,
    f_send,
    f_recv,
    b_send,
    b_recv,
    sib_send,
    sib_recv,
    rs_send,
    rs_recv,
    y_send,
    y_recv,
    ag_send,
    ag_recv,
    fw_send,
    fw_recv,
    gs_sem,
    gy_sem,
    gz_send,
    gz_recv,
):
    features = wm.shape[-1]
    s = lax.axis_index("section")
    dp = lax.axis_index("dp")
    core = lax.rem(dp, CORES)
    z = lax.rem(dp // CORES, RING)
    yh = dp // (CORES * RING)
    first = s == 0
    last = s == sections - 1
    not_first = s > 0
    not_last = s < sections - 1

    def dp_at(y_, z_, c_):
        return {"dp": (y_ * RING + z_) * CORES + c_}

    sibling = dp_at(yh, z, 1 - core)
    across = dp_at(1 - yh, z, core)
    z_next = lax.rem(z + 1, RING)
    z_prev = lax.rem(z + RING - 1, RING)

    barrier = pltpu.get_barrier_semaphore()

    def greet(where):
        pl.semaphore_signal(barrier, inc=1, device_id=where, device_id_type=MESH)

    @pl.when(not_first)
    def _():
        greet({"section": s - 1})

    @pl.when(not_last)
    def _():
        greet({"section": s + 1})

    greet(sibling)
    greet(across)
    for d in range(1, RING):
        greet(dp_at(yh, lax.rem(z + d, RING), core))

    loads = [
        pltpu.make_async_copy(a, b, in_sem.at[i])
        for i, (a, b) in enumerate(
            [
                (g2m_hbm, g2m),
                (m2m_hbm, m2m),
                (wm_hbm.at[0], wm),
                (wu_hbm.at[0], wu),
                (wd_hbm.at[0], wd),
                (gain_hbm, gain_v),
                (m2g_hbm, m2g),
            ]
        )
    ]

    def lat_load(j):
        return pltpu.make_async_copy(lat_hbm.at[j], lat.at[j], lat_sem.at[j])

    def tgt_load(j):
        return pltpu.make_async_copy(tgt_hbm.at[j], tgt.at[j], tgt_sem.at[j])

    loads[0].start()

    @pl.when(first)
    def _():
        for j in range(samples):
            lat_load(j).start()

    for load in loads[1:]:
        load.start()

    @pl.when(last)
    def _():
        for j in range(samples):
            tgt_load(j).start()

    acc[...] = jnp.zeros_like(acc)
    gacc[...] = jnp.zeros_like(gacc)

    for load in loads:
        load.wait()

    def kept_if(col, b, tile):
        return jnp.where(jnp.full(tile.shape, col, jnp.int32) == b, tile, jnp.zeros_like(tile))

    for k in range(2):
        for r in range(2):
            tile = m2m[2 * r + k]
            for b in range(2):
                kept = kept_if(m2m_c[2 * r + k], b, tile)
                mix[r * BLOCK : (r + 1) * BLOCK, (2 * k + b) * BLOCK : (2 * k + b + 1) * BLOCK] = kept
                mix_t[b * BLOCK : (b + 1) * BLOCK, (2 * k + r) * BLOCK : (2 * k + r + 1) * BLOCK] = kept.T

    @pl.when(first)
    def _():
        for t in range(4):
            for b in range(4):
                k, r = t % 2, t // 2
                kept = kept_if(g2m_c[t], b, g2m[t])
                enc[r * BLOCK : (r + 1) * BLOCK, (4 * k + b) * BLOCK : (4 * k + b + 1) * BLOCK] = kept

    @pl.when(last)
    def _():
        for t in range(8):
            tile_t = m2g[t].T
            for b in range(2):
                k, r = t % 2, t // 2
                kept = kept_if(m2g_c[t], b, m2g[t])
                pred[r * BLOCK : (r + 1) * BLOCK, (2 * k + b) * BLOCK : (2 * k + b + 1) * BLOCK] = kept
                kept = kept_if(m2g_c[t], b, tile_t)
                seed_t[b * BLOCK : (b + 1) * BLOCK, (4 * k + r) * BLOCK : (4 * k + r + 1) * BLOCK] = kept

    pl.semaphore_wait(
        barrier, RING + 1 + jnp.where(first, 0, 1) + jnp.where(last, 0, 1)
    )

    span = NODES // CHUNKS

    def rows_of(c):
        return pl.ds(c * span, span)

    def send_f(j, c):
        return pltpu.make_async_remote_copy(
            src_ref=xout.at[j, rows_of(c)],
            dst_ref=xin.at[j, rows_of(c)],
            send_sem=f_send.at[j, c],
            recv_sem=f_recv.at[j, c],
            device_id={"section": jnp.minimum(s + 1, sections - 1)},
            device_id_type=MESH,
        )

    def send_b(j, c):
        return pltpu.make_async_remote_copy(
            src_ref=gout.at[j, rows_of(c)],
            dst_ref=gin.at[j, rows_of(c)],
            send_sem=b_send.at[j, c],
            recv_sem=b_recv.at[j, c],
            device_id={"section": jnp.maximum(s - 1, 0)},
            device_id_type=MESH,
        )

    def forward(j):
        @pl.when(first)
        def _():
            lat_load(j).wait()
            grid_rows = lat.shape[1]
            xin[j] = (dot(enc[:, :grid_rows], lat[j]) + dot(enc[:, grid_rows:], lat[j])).astype(BF16)

        gain = gain_v[...]
        for c in range(CHUNKS):
            rows = rows_of(c)

            @pl.when(not_first)
            def _():
                send_f(j, c).wait_recv()

            x = xin[j, rows, :].astype(F32)
            center = x - jnp.mean(x, axis=-1, keepdims=True)
            inverse = lax.rsqrt(jnp.mean(center * center, axis=-1, keepdims=True) + EPSILON)
            normed = center * inverse
            unit = (normed * gain).astype(BF16)
            normed_s[j, rows, :] = normed
            inv_s[j, rows, :] = jnp.broadcast_to(inverse, (span, 128))
            unit_s[rows, :] = unit
            msg = dot(unit, wm[...]).astype(BF16)
            for k in range(2):
                msg_s[pl.ds(k * NODES + c * span, span), :] = msg
            up_s[rows, :] = dot(unit, wu[...])
        for c in range(CHUNKS):
            rows = rows_of(c)
            before = up_s[rows, :] + dot(mix[rows, :], msg_s[...])
            sigma = 1.0 / (1.0 + jnp.exp(-before))
            active = (before * sigma).astype(BF16)
            slope_s[j, rows, :] = sigma * (1.0 + before * (1.0 - sigma))
            gb_s[rows, :] = active
            output = xin[j, rows, :].astype(F32) + dot(active, wd[...])
            xout[j, rows, :] = output.astype(BF16)

            @pl.when(not_last)
            def _():
                send_f(j, c).start()

        unit_t[j] = unit_s[...].T
        act_t[j] = gb_s[pl.ds(0, NODES), :].T

        @pl.when(last)
        def _():
            tgt_load(j).wait()
            upstream = jnp.zeros((NODES, features), F32)
            for r in range(4):
                here = pl.ds(r * BLOCK, BLOCK)
                predicted = dot(pred[here, :NODES], xout[j]) + dot(pred[here, NODES:], xout[j])
                target = tgt[j, r * BLOCK : (r + 1) * BLOCK, :].astype(F32)
                residual = ((predicted - target) * loss_scale).astype(BF16)
                for k in range(2):
                    part = seed_t[:, (4 * k + r) * BLOCK : (4 * k + r + 1) * BLOCK]
                    upstream = upstream + dot(part, residual)
            gin[j] = upstream.astype(BF16)

    def backward(j):
        gain = gain_v[...]
        for c in range(CHUNKS):
            rows = rows_of(c)

            @pl.when(not_last)
            def _():
                send_b(j, c).wait_recv()

            grad_active = dot_nt(gin[j, rows, :], wd[...])
            grad_before = (grad_active * slope_s[j, rows, :]).astype(BF16)
            for k in range(2):
                gb_s[pl.ds(k * NODES + c * span, span), :] = grad_before
        gm_s[...] = dot(mix_t[...], gb_s[...]).astype(BF16)
        for c in range(CHUNKS):
            rows = rows_of(c)
            grad_unit = dot_nt(gb_s[rows, :], wu[...]) + dot_nt(gm_s[rows, :], wm[...])
            normed = normed_s[j, rows, :]
            product = grad_unit * normed
            gacc[...] = gacc[...] + jnp.sum(product.reshape(span // 8, 8, features), axis=0)

            @pl.when(not_first)
            def _():
                grad_normed = grad_unit * gain
                inverse = inv_s[j, rows, :][:, :1]
                grad_inputs = gin[j, rows, :].astype(F32) + inverse * (
                    grad_normed
                    - jnp.mean(grad_normed, axis=-1, keepdims=True)
                    - normed * jnp.mean(grad_normed * normed, axis=-1, keepdims=True)
                )
                gout[j, rows, :] = grad_inputs.astype(BF16)
                send_b(j, c).start()

        acc[0:features, :] += dot(unit_t[j], gm_s[...])
        acc[features : 2 * features, :] += dot(unit_t[j], gb_s[pl.ds(0, NODES), :])
        acc[2 * features :, :] += dot(act_t[j], gin[j])

    @pl.loop(0, 2 * samples)
    def _(t):
        going_back = jnp.where(last, lax.rem(t, 2), t // samples)
        j = jnp.where(last, t // 2, lax.rem(t, samples))

        @pl.when(going_back == 0)
        def _():
            forward(j)

        @pl.when(going_back == 1)
        def _():
            backward(j)

    half = acc.shape[0] // CORES
    arm = half // 2
    piece = arm // RING
    sub = piece // SUBS

    def remote(src, dst, send, recv, where):
        return pltpu.make_async_remote_copy(
            src_ref=src, dst_ref=dst, send_sem=send, recv_sem=recv, device_id=where, device_id_type=MESH
        )

    def arm_rows(c, d):
        return pl.ds(pl.multiple_of(c * half + d * arm, 8), arm)

    def sub_rows(d, chunk, u):
        return pl.ds(pl.multiple_of(core * half + d * arm + chunk * piece + u * sub, 8), sub)

    def piece_rows(d, chunk):
        return pl.ds(pl.multiple_of(core * half + d * arm + chunk * piece, 16), piece)

    def to_sib(d):
        return remote(acc.at[arm_rows(1 - core, d)], sib_buf.at[d], sib_send.at[d], sib_recv.at[d], sibling)

    g_to_sib = remote(gacc, g_sib, gs_sem.at[0], gs_sem.at[1], sibling)
    g_to_sib.start()
    for d in range(2):
        to_sib(d).start()

    def toward(d):
        return dp_at(yh, z_next if d == 0 else z_prev, core)

    def chunk_at(d, shift):
        return lax.rem(z - shift + 2 * RING, RING) if d == 0 else lax.rem(z + shift, RING)

    def rs(d, t, u):
        rows = sub_rows(d, chunk_at(d, t + 1), u)
        return remote(acc.at[rows], ring_buf.at[d, t, u], rs_send.at[d, t, u], rs_recv.at[d, t, u], toward(d))

    def y_copy(d, u):
        return remote(acc.at[sub_rows(d, z, u)], y_buf.at[d, u], y_send.at[d, u], y_recv.at[d, u], across)

    for d in range(2):
        to_sib(d).wait()
        rows = arm_rows(core, d)
        acc[rows, :] += sib_buf[d]
        for u in range(SUBS):
            rs(d, 0, u).start()

    g_to_sib.wait()
    gacc[...] += g_sib[...]
    g_to_y = remote(gacc, g_y, gy_sem.at[0], gy_sem.at[1], across)
    g_to_y.start()

    @pl.loop(0, STEPS)
    def _(t):
        for u in range(SUBS):
            for d in range(2):
                rs(d, t, u).wait_recv()
                rows = sub_rows(d, chunk_at(d, t + 2), u)
                acc[rows, :] += ring_buf[d, t, u]

                @pl.when(t < STEPS - 1)
                def _():
                    rs(d, t + 1, u).start()

                @pl.when(t == STEPS - 1)
                def _():
                    y_copy(d, u).start()

    def all_gather(d, t):
        rows = piece_rows(d, chunk_at(d, t))
        return remote(out.at[rows], out.at[rows], ag_send.at[d, t], ag_recv.at[d, t], toward(d))

    def all_gather_in(d, t):
        rows = piece_rows(d, chunk_at(d, t + 1))
        return remote(out.at[rows], out.at[rows], ag_send.at[d, t], ag_recv.at[d, t], toward(d))

    def hand_over(d, t):
        rows = piece_rows(d, chunk_at(d, t))
        return remote(out.at[rows], out.at[rows], fw_send.at[d, t], fw_recv.at[d, t], sibling)

    g_to_y.wait()
    g_z[z] = gacc[...] + g_y[...]

    def g_spread(d):
        return remote(g_z.at[z], g_z.at[z], gz_send.at[d - 1], gz_recv.at[d - 1], dp_at(yh, lax.rem(z + d, RING), core))

    def g_arrive(d):
        at = lax.rem(z - d + RING, RING)
        return remote(g_z.at[at], g_z.at[at], gz_send.at[d - 1], gz_recv.at[d - 1], dp_at(yh, at, core))

    for d in range(1, RING):
        g_spread(d).start()

    for d in range(2):
        for u in range(SUBS):
            y_copy(d, u).wait()
        total = acc[piece_rows(d, z), :] + y_buf[d].reshape(piece, features)
        out[piece_rows(d, z), :] = total.astype(BF16)
        all_gather(d, 0).start()
        hand_over(d, 0).start()

    @pl.loop(0, STEPS)
    def _(t):
        for d in range(2):
            all_gather_in(d, t).wait_recv()

            @pl.when(t < STEPS - 1)
            def _():
                all_gather(d, t + 1).start()

            hand_over(d, t + 1).start()

    for d in range(1, RING):
        g_arrive(d).wait_recv()
    total = g_z[0]
    for i in range(1, RING):
        total = total + g_z[i]
    gain_out[...] = jnp.broadcast_to(jnp.sum(total, axis=0, keepdims=True), gain_out.shape)

    def hand_over_in(d, t):
        at = pl.ds(pl.multiple_of((1 - core) * half + d * arm + chunk_at(d, t) * piece, 16), piece)
        return remote(out.at[at], out.at[at], fw_send.at[d, t], fw_recv.at[d, t], sibling)

    @pl.loop(0, RING)
    def _(t):
        for d in range(2):
            hand_over_in(d, t).wait_recv()
            hand_over(d, t).wait_send()

    @pl.loop(0, STEPS)
    def _(t):
        for d in range(2):
            all_gather(d, t).wait_send()
            for u in range(SUBS):
                rs(d, t, u).wait_send()

    for d in range(1, RING):
        g_spread(d).wait_send()

    @pl.loop(0, samples)
    def _(j):
        for c in range(CHUNKS):

            @pl.when(not_last)
            def _():
                send_f(j, c).wait_send()

            @pl.when(not_first)
            def _():
                send_b(j, c).wait_send()


def on_device(sections, replicas, *args):
    lat, tgt, g2m, g2m_c, m2m, m2m_c, m2g, m2g_c, wm, wu, wd, gains = args
    samples, grid_rows, features = lat.shape
    halves = replicas // (CORES * RING)
    loss_scale = 1.0 / math.sqrt(samples * replicas * grid_rows)
    any_spec = pl.BlockSpec(memory_space=pl.ANY)
    smem_spec = pl.BlockSpec(memory_space=pltpu.SMEM)
    vmem_spec = pl.BlockSpec(memory_space=pltpu.VMEM)
    total_rows = 3 * features
    piece = total_rows // CORES // 2 // RING
    dma = pltpu.SemaphoreType.DMA
    v = pltpu.VMEM
    tile = (BLOCK, BLOCK)
    per_sample = (samples, NODES, features)
    out, gain_out = pl.pallas_call(
        functools.partial(step_kernel, sections, halves, samples, loss_scale),
        out_shape=(
            jax.ShapeDtypeStruct((total_rows, features), BF16),
            jax.ShapeDtypeStruct((8, features), F32),
        ),
        in_specs=[any_spec, any_spec, any_spec, smem_spec, any_spec, smem_spec, any_spec, smem_spec]
        + [any_spec] * 4,
        out_specs=(vmem_spec, vmem_spec),
        scratch_shapes=[
            v((samples, grid_rows, features), BF16),
            v((samples, grid_rows, features), BF16),
            v((4,) + tile, BF16),
            v((4,) + tile, BF16),
            v((8,) + tile, BF16),
            v((features, features), BF16),
            v((features, features), BF16),
            v((features, features), BF16),
            v((1, features), F32),
            v((NODES, 2 * NODES), BF16),
            v((NODES, 2 * NODES), BF16),
            v((NODES, 2 * grid_rows), BF16),
            v((grid_rows, 2 * NODES), BF16),
            v((NODES, 2 * grid_rows), BF16),
            v(per_sample, BF16),
            v(per_sample, BF16),
            v(per_sample, BF16),
            v(per_sample, BF16),
            v((NODES, features), BF16),
            v((samples, features, NODES), BF16),
            v((samples, features, NODES), BF16),
            v(per_sample, F32),
            v(per_sample, F32),
            v((samples, NODES, 128), F32),
            v((2 * NODES, features), BF16),
            v((NODES, features), F32),
            v((2 * NODES, features), BF16),
            v((NODES, features), BF16),
            v((total_rows, features), F32),
            v((8, features), F32),
            v((2, total_rows // CORES // 2, features), F32),
            v((2, STEPS, SUBS, piece // SUBS, features), F32),
            v((2, SUBS, piece // SUBS, features), F32),
            v((8, features), F32),
            v((8, features), F32),
            v((RING, 8, features), F32),
            dma((7,)),
            dma((samples,)),
            dma((samples,)),
            dma((samples, CHUNKS)),
            dma((samples, CHUNKS)),
            dma((samples, CHUNKS)),
            dma((samples, CHUNKS)),
            dma((2,)),
            dma((2,)),
            dma((2, STEPS, SUBS)),
            dma((2, STEPS, SUBS)),
            dma((2, SUBS)),
            dma((2, SUBS)),
            dma((2, STEPS)),
            dma((2, STEPS)),
            dma((2, RING)),
            dma((2, RING)),
            dma((2,)),
            dma((2,)),
            dma((STEPS,)),
            dma((STEPS,)),
        ],
        compiler_params=pltpu.CompilerParams(
            collective_id=0, has_side_effects=True, vmem_limit_bytes=48 * 1024 * 1024
        ),
        name="train_step",
    )(*args)
    weight_grads = out.astype(F32).reshape(1, 3, features, features)
    return weight_grads, gain_out[:1]


def solution(mesh):
    placed = (
        P("dp", None, None),
        P("dp", None, None),
        P(),
        P(),
        P(),
        P(),
        P(),
        P(),
        P("section", None, None),
        P("section", None, None),
        P("section", None, None),
        P("section", None),
    )
    return jax.shard_map(
        functools.partial(on_device, mesh.shape["section"], mesh.shape["dp"]),
        mesh=mesh,
        in_specs=placed,
        out_specs=(P("section", None, None, None), P("section", None)),
        check_vma=False,
    )
```

time: 726 us -> 214 us (0.29)
  waiting for transfers between devices: 436 us -> 0 us
  Pallas kernels: 0 us -> 201 us
  blocking collectives: 92.3 us -> 0 us
  starting transfers between devices: 79.6 us -> 0 us
  matrix products: 54.6 us -> 0 us
  other arithmetic: 20.6 us -> 2.11 us
  local copies, waits for them, and re-layouts: 26.4 us -> 10.5 us
  between operations: 14.1 us -> 0.66 us
    ppermute x20 -> x0, waiting for transfers between devices: 228 us -> none  [shifted(): return lax.ppermute(block, axis, route)]
    psum x1 -> x0, waiting for transfers between devices: 207 us -> none  [on_device(): summed = lax.psum((totals[0], totals[1], totals[2], totals[3]), 'dp')]
    pallas_call x0 -> x1, Pallas kernels: none -> 201 us  [on_device(): pl.pallas_call(functools.partial(step_kernel, sections, halves, samples,...]
    psum x1 -> x0, blocking collectives: 92.3 us -> none  [on_device(): summed = lax.psum((totals[0], totals[1], totals[2], totals[3]), 'dp')]
    ppermute x20 -> x0, starting transfers between devices: 79.5 us -> none  [shifted(): return lax.ppermute(block, axis, route)]
    dot_general x42 -> x0, matrix products: 54.6 us -> none  [the longest x6 8.59 us: layer_forward(): jnp.dot(unit, w_m, preferred_element_type=jnp.float32).astype(jnp.bfloat16)]
    broadcast_in_dim x52 -> x0, local copies, waits for them, and re-layouts: 19.7 us -> none  [the longest x16 10.9 us: on_device(): zero_rows = jnp.zeros((NODES, features), jnp.bfloat16)]
  transfers between devices with their start and end apart: 21 -> 0, of which waited for: 21 -> 0; matrix products, arithmetic and copies ran while one was open for 0% -> 0% of each run, Pallas kernels for 0% -> 0%
where the time goes in v1:
time: 214 us
  Pallas kernels  201 us (94%)
  local copies, waits for them, and re-layouts  10.5 us (5%)
    pallas_call x1, Pallas kernels, on_device(): pl.pallas_call(functools.partial(step_kernel, sections, halves, samples,...  201 us
    unnamed x22, local copies, waits for them, and re-layouts  9.93 us

profile of v1, /device:TPU:1, one launch (start us, length us, event | category | flops | bytes accessed | tf_op | source)
XLA Modules:
  0.0 214.0 jit_solution(18304278804713266594)
XLA Ops:
  0.6 0.0 copy-start
  0.6 1.4 copy-done
  2.0 0.0 copy-start.1
  2.0 1.0 copy-done.1
  3.1 0.0 copy-start.2
  3.1 1.0 copy-done.2
  4.1 0.0 copy-start.3
  4.1 1.0 copy-done.3
  5.2 0.0 copy-start.4
  5.2 0.9 copy-done.4
  6.1 0.0 copy-start.5
  6.1 0.9 copy-done.5
  7.0 0.0 copy-start.6
  7.0 0.9 copy-done.6
  7.9 0.0 copy-start.7
  7.9 0.7 copy-done.7
  8.6 0.0 copy-start.8
  8.6 0.7 copy-done.8
  9.3 0.0 copy-start.9
  9.3 0.7 copy-done.9
  9.9 0.0 copy-start.10
  9.9 0.7 copy-done.10
  10.6 200.7 %train_step.1 = (bf16[1536,512]{1,0:T(8,128)(2,1)S(1)}, f32[8,512]{1,0:T(8,128)S(1)}) custom-call(bf16[3,512,512]{2,1,0:T(8,128)(2,1)S(1)} %copy-done, bf16[3,512,512]{2,1,0:T(8,128)(2,1)} %tgt_hbm.1, bf16[4,128,128]{2,1,0:T(8,128)(2,1)S(1)} %copy-done.5, s32[4]{0:T(128)S(1)} %copy-done.8, bf16[4,128,128]{2,1,0:T(8,128)(2,1)S(1)} %copy-done.6, ...), custom_call_target="tpu_custom_call" | custom-call | tf_op jit(solution)/shard_map/train_step/pallas_call | solution.py:521
  211.3 0.6 slice.3
  211.9 2.1 convert.1
Async XLA Ops:
  0.6 1.4 copy-start
  2.0 1.0 copy-start.1
  3.1 1.0 copy-start.2
  4.1 1.0 copy-start.3
  5.2 0.9 copy-start.4
  6.1 0.9 copy-start.5
  7.0 0.9 copy-start.6
  7.9 0.7 copy-start.7
  8.6 0.7 copy-start.8
  9.3 0.7 copy-start.9
  9.9 0.7 copy-start.10

commit v2 on v1

v2 whole, which is shorter than its diff:
```python
import functools
import math

import jax
import jax.numpy as jnp
from jax import lax
from jax.experimental import pallas as pl
from jax.experimental.pallas import tpu as pltpu
from jax.sharding import PartitionSpec as P

BLOCK = 128
NODES = 256
EPSILON = 1e-05
MESH = pl.DeviceIdType.MESH
F32 = jnp.float32
BF16 = jnp.bfloat16
CHUNKS = 2
LAYERS = 4
CORES = 2
RING = 8
STEPS = RING - 1
FAR = RING // 2
SUM = True


def dot(a, b):
    return jnp.dot(a, b, preferred_element_type=F32)


def dot_nt(a, b):
    return lax.dot_general(a, b, (((1,), (1,)), ((), ())), preferred_element_type=F32)


def step_kernel(
    samples,
    loss_scale,
    lat_hbm,
    tgt_hbm,
    g2m_hbm,
    g2m_c_hbm,
    m2m_hbm,
    m2m_c_hbm,
    m2g_hbm,
    m2g_c_hbm,
    wm_hbm,
    wu_hbm,
    wd_hbm,
    gain_hbm,
    out,
    gain_out,
    lat,
    tgt,
    g2m,
    m2m,
    m2g,
    g2m_c,
    m2m_c,
    m2g_c,
    w,
    gain_v,
    gains,
    mix,
    mix_t,
    enc,
    pred,
    seed_t,
    h,
    up,
    unit_s,
    act_s,
    gb_s,
    gp_s,
    slope_s,
    normed_s,
    inv_s,
    msg_s,
    up_s,
    gm_s,
    unit_t,
    act_t,
    acc,
    gacc,
    sib_buf,
    ring_buf,
    y_buf,
    g_sib,
    g_y,
    g_z,
    in_sem,
    io_sem,
    wt_send,
    wt_recv,
    ws_send,
    ws_recv,
    gn_send,
    gn_recv,
    hop_send,
    hop_recv,
    pass_send,
    pass_recv,
    sib_send,
    sib_recv,
    rs_send,
    rs_recv,
    y_send,
    y_recv,
    ag_send,
    ag_recv,
    fw_send,
    fw_recv,
    gs_sem,
    gy_sem,
    gz_send,
    gz_recv,
):
    features = w.shape[-1]
    s = lax.axis_index("section")
    dp = lax.axis_index("dp")
    core = lax.rem(dp, CORES)
    z = lax.rem(dp // CORES, RING)
    yh = dp // (CORES * RING)
    stage = s // LAYERS
    m = lax.rem(s, LAYERS)
    mx, my = m // 2, lax.rem(m, 2)
    early = stage == 0
    late = stage == 1
    j = jnp.where(early, m, 2 * (1 - mx) + my)
    busy = j < samples

    def dp_at(y_, z_, c_):
        return {"dp": (y_ * RING + z_) * CORES + c_}

    def relative(k):
        x_ = lax.rem(mx + k // 2, 2)
        y_ = lax.rem(my + k % 2, 2)
        return 2 * x_ + y_

    y_cross = lax.rem(yh + core, 2)

    def member_at(layer):
        y_ = jnp.where(lax.rem(layer, 2) == my, yh, y_cross)
        return {"section": LAYERS * stage + layer, "dp": (y_ * RING + z) * CORES + core}

    hop_to = {"section": 2 * (3 - s // 2) + lax.rem(s, 2)}
    sibling = dp_at(yh, z, 1 - core)
    across = dp_at(1 - yh, z, core)
    z_next = lax.rem(z + 1, RING)
    z_prev = lax.rem(z + RING - 1, RING)

    def remote(src, dst, send, recv, where):
        return pltpu.make_async_remote_copy(
            src_ref=src, dst_ref=dst, send_sem=send, recv_sem=recv, device_id=where, device_id_type=MESH
        )

    barrier = pltpu.get_barrier_semaphore()

    def greet(where):
        pl.semaphore_signal(barrier, inc=1, device_id=where, device_id_type=MESH)

    greet(sibling)
    for k in (1, 2, 3):
        greet(member_at(relative(k)))
    greet(hop_to)
    met = 5
    if SUM:
        greet(across)
        for d in range(1, RING):
            greet(dp_at(yh, lax.rem(z + d, RING), core))
        met += RING

    w_hbm = (wm_hbm, wu_hbm, wd_hbm)
    loads = [
        pltpu.make_async_copy(a, b, in_sem.at[i])
        for i, (a, b) in enumerate(
            [
                (g2m_c_hbm, g2m_c),
                (m2m_c_hbm, m2m_c),
                (m2g_c_hbm, m2g_c),
                (g2m_hbm, g2m),
                (m2m_hbm, m2m),
                (gain_hbm, gain_v),
                (m2g_hbm, m2g),
            ]
            + [(w_hbm[i].at[0], w.at[i, m]) for i in range(3)]
        )
    ]
    sample = jnp.minimum(j, samples - 1)
    lat_load = pltpu.make_async_copy(lat_hbm.at[sample], lat, io_sem.at[0])
    tgt_load = pltpu.make_async_copy(tgt_hbm.at[sample], tgt, io_sem.at[1])
    for load in loads:
        load.start()
    lat_load.start()
    tgt_load.start()

    def half_of(i, layer, c):
        rows = features // 2
        return w.at[i, layer, pl.ds(pl.multiple_of(c * rows, 16), rows)]

    def give(k, i):
        if k == 3:
            layer, where = relative(2), member_at(relative(1))
        else:
            layer, where = m, member_at(relative(k))
        rows = features // 2
        here = half_of(i, layer, core)
        src = here if k == 3 else w_hbm[i].at[0, pl.ds(pl.multiple_of(core * rows, 16), rows)]
        return remote(src, here, wt_send.at[k - 1, i], wt_recv.at[k - 1, i], where)

    def got(k, i):
        here = half_of(i, relative(k), core)
        return remote(here, here, wt_send.at[k - 1, i], wt_recv.at[k - 1, i], sibling)

    def share(k, i):
        here = half_of(i, relative(k), core)
        return remote(here, here, ws_send.at[k - 1, i], ws_recv.at[k - 1, i], sibling)

    def shared(k, i):
        here = half_of(i, relative(k), 1 - core)
        return remote(here, here, ws_send.at[k - 1, i], ws_recv.at[k - 1, i], sibling)

    def give_gain(k):
        return remote(gains.at[m], gains.at[m], gn_send.at[k - 1], gn_recv.at[k - 1], member_at(relative(k)))

    def got_gain(k):
        here = gains.at[relative(k)]
        return remote(here, here, gn_send.at[k - 1], gn_recv.at[k - 1], sibling)

    pl.semaphore_wait(barrier, met)
    for i in range(3):
        for k in (1, 2):
            give(k, i).start()
    for load in loads:
        load.wait()
    gains[m] = jnp.broadcast_to(gain_v[...], (8, features))
    for k in (1, 2, 3):
        give_gain(k).start()

    def kept_if(col, b, tile):
        return jnp.where(jnp.full(tile.shape, col, jnp.int32) == b, tile, jnp.zeros_like(tile))

    for k in range(2):
        for r in range(2):
            tile = m2m[2 * r + k]
            for b in range(2):
                kept = kept_if(m2m_c[2 * r + k], b, tile)
                mix[r * BLOCK : (r + 1) * BLOCK, (2 * k + b) * BLOCK : (2 * k + b + 1) * BLOCK] = kept
                mix_t[b * BLOCK : (b + 1) * BLOCK, (2 * k + r) * BLOCK : (2 * k + r + 1) * BLOCK] = kept.T

    lat_load.wait()
    tgt_load.wait()

    @pl.when(early)
    def _():
        for t in range(4):
            for b in range(4):
                k, r = t % 2, t // 2
                kept = kept_if(g2m_c[t], b, g2m[t])
                enc[r * BLOCK : (r + 1) * BLOCK, (4 * k + b) * BLOCK : (4 * k + b + 1) * BLOCK] = kept

    @pl.when(late)
    def _():
        for t in range(8):
            tile_t = m2g[t].T
            for b in range(2):
                k, r = t % 2, t // 2
                kept = kept_if(m2g_c[t], b, m2g[t])
                pred[r * BLOCK : (r + 1) * BLOCK, (2 * k + b) * BLOCK : (2 * k + b + 1) * BLOCK] = kept
                kept = kept_if(m2g_c[t], b, tile_t)
                seed_t[b * BLOCK : (b + 1) * BLOCK, (4 * k + r) * BLOCK : (4 * k + r + 1) * BLOCK] = kept

    span = NODES // CHUNKS

    def rows_of(c):
        return pl.ds(c * span, span)

    def hop_f(c):
        return remote(h.at[LAYERS, rows_of(c)], h.at[0, rows_of(c)], hop_send.at[0, c], hop_recv.at[0, c], hop_to)

    def hop_b(c):
        return remote(up.at[0, rows_of(c)], up.at[LAYERS, rows_of(c)], hop_send.at[1, c], hop_recv.at[1, c], hop_to)

    kinds = ((unit_s, 0), (act_s, 0), (up, 1), (gb_s, 0), (gp_s, 0))

    def hand_in(layer, i):
        ref, shift = kinds[i]
        return remote(
            ref.at[layer + shift], ref.at[LAYERS + shift + j], pass_send.at[layer, i], pass_recv.at[j, i], member_at(layer)
        )

    def handed_in(from_j, i):
        ref, shift = kinds[i]
        here = ref.at[LAYERS + shift + from_j]
        return remote(here, here, pass_send.at[0, i], pass_recv.at[from_j, i], sibling)

    def forward(l):
        @pl.when(early & (l == 0))
        def _():
            grid_rows = lat.shape[0]
            h[0] = (dot(enc[:, :grid_rows], lat[...]) + dot(enc[:, grid_rows:], lat[...])).astype(BF16)

        gain = gains[l, 0:1, :]
        for c in range(CHUNKS):
            rows = rows_of(c)

            @pl.when(late & (l == 0))
            def _():
                hop_f(c).wait_recv()

            x = h[l, rows, :].astype(F32)
            center = x - jnp.mean(x, axis=-1, keepdims=True)
            inverse = lax.rsqrt(jnp.mean(center * center, axis=-1, keepdims=True) + EPSILON)
            normed = center * inverse
            unit = (normed * gain).astype(BF16)
            normed_s[l, rows, :] = normed
            inv_s[l, rows, :] = jnp.broadcast_to(inverse, (span, 128))
            unit_s[l, rows, :] = unit
            msg_s[rows, :] = dot(unit, w[0, l]).astype(BF16)
            up_s[rows, :] = dot(unit, w[1, l])
        for c in range(CHUNKS):
            rows = rows_of(c)
            before = up_s[rows, :] + dot(mix[rows, :NODES], msg_s[...]) + dot(mix[rows, NODES:], msg_s[...])
            sigma = 1.0 / (1.0 + jnp.exp(-before))
            active = (before * sigma).astype(BF16)
            slope_s[l, rows, :] = sigma * (1.0 + before * (1.0 - sigma))
            act_s[l, rows, :] = active
            output = h[l, rows, :].astype(F32) + dot(active, w[2, l])
            h[l + 1, rows, :] = output.astype(BF16)

            @pl.when(early & (l == LAYERS - 1))
            def _():
                hop_f(c).start()

        @pl.when(l != m)
        def _():
            hand_in(l, 0).start()
            hand_in(l, 1).start()

        @pl.when(late & (l == LAYERS - 1))
        def _():
            upstream = jnp.zeros((NODES, features), F32)
            for r in range(4):
                here = pl.ds(r * BLOCK, BLOCK)
                predicted = dot(pred[here, :NODES], h[LAYERS]) + dot(pred[here, NODES:], h[LAYERS])
                target = tgt[r * BLOCK : (r + 1) * BLOCK, :].astype(F32)
                residual = ((predicted - target) * loss_scale).astype(BF16)
                for k in range(2):
                    part = seed_t[:, (4 * k + r) * BLOCK : (4 * k + r + 1) * BLOCK]
                    upstream = upstream + dot(part, residual)
            up[LAYERS] = upstream.astype(BF16)

    def backward(l):
        gain = gains[l, 0:1, :]
        for c in range(CHUNKS):
            rows = rows_of(c)

            @pl.when(early & (l == LAYERS - 1))
            def _():
                hop_b(c).wait_recv()

            grad_active = dot_nt(up[l + 1, rows, :], w[2, l])
            gb_s[l, rows, :] = (grad_active * slope_s[l, rows, :]).astype(BF16)

        @pl.when(l != m)
        def _():
            hand_in(l, 2).start()
            hand_in(l, 3).start()

        gm_s[...] = (dot(mix_t[:, :NODES], gb_s[l]) + dot(mix_t[:, NODES:], gb_s[l])).astype(BF16)
        for c in range(CHUNKS):
            rows = rows_of(c)
            grad_unit = dot_nt(gb_s[l, rows, :], w[1, l]) + dot_nt(gm_s[rows, :], w[0, l])
            normed = normed_s[l, rows, :]
            part = jnp.sum((grad_unit * normed).reshape(span // 8, 8, features), axis=0)
            gp_s[l] = part if c == 0 else gp_s[l] + part

            @pl.when(late | (l > 0))
            def _():
                grad_normed = grad_unit * gain
                inverse = inv_s[l, rows, :][:, :1]
                grad_inputs = up[l + 1, rows, :].astype(F32) + inverse * (
                    grad_normed
                    - jnp.mean(grad_normed, axis=-1, keepdims=True)
                    - normed * jnp.mean(grad_normed * normed, axis=-1, keepdims=True)
                )
                up[l, rows, :] = grad_inputs.astype(BF16)

            @pl.when(late & (l == 0))
            def _():
                hop_b(c).start()

        @pl.when(l != m)
        def _():
            hand_in(l, 4).start()

    def round_of(l):
        last = 0
        for i in range(LAYERS):
            far = 2 * lax.rem(i // 2 + mx, 2) + lax.rem(i % 2 + my, 2)
            last = jnp.maximum(last, jnp.where(l >= i, far, 0))
        return jnp.where(early, last, LAYERS - 1)

    @pl.loop(0, LAYERS * LAYERS)
    def _(t):
        e, l = t // LAYERS, lax.rem(t, LAYERS)

        @pl.when((e == 1) & (l == 0))
        def _():
            for k in (1, 2, 3):
                got_gain(k).wait_recv()
            for k, i in ((1, 0), (1, 1), (2, 0), (1, 2)):
                got(k, i).wait_recv()
                if k == 2:
                    give(3, i).start()
                share(k, i).start()
            for i in range(3):
                shared(1, i).wait_recv()

        @pl.when((e == 2) & (l == 0))
        def _():
            for i in (1, 2):
                got(2, i).wait_recv()
                give(3, i).start()
                share(2, i).start()
            for i in range(3):
                shared(2, i).wait_recv()

        @pl.when((e == 3) & (l == 0))
        def _():
            for i in range(3):
                got(3, i).wait_recv()
                share(3, i).start()
            for i in range(3):
                shared(3, i).wait_recv()

        @pl.when(busy & (round_of(l) == e))
        def _():
            forward(l)

    def turn():
        @pl.loop(0, samples)
        def _(i):
            mine = i == j

            @pl.when(jnp.logical_not(mine))
            def _():
                handed_in(i, 0).wait_recv()
                handed_in(i, 1).wait_recv()

            at = jnp.where(mine, m, LAYERS + i)
            unit_t[i] = unit_s[at].T
            act_t[i] = act_s[at].T

    @pl.when(early)
    def _():
        turn()

    @pl.loop(0, LAYERS)
    def _(t):
        @pl.when(busy)
        def _():
            backward(LAYERS - 1 - t)

    @pl.when(late)
    def _():
        turn()

    @pl.loop(0, samples)
    def _(t):
        i = lax.rem(j + t, samples)
        mine = i == j

        @pl.when(jnp.logical_not(mine))
        def _():
            for kind in (2, 3, 4):
                handed_in(i, kind).wait_recv()

        at = jnp.where(mine, m, LAYERS + i)
        grad_before = gb_s[at]
        gm_s[...] = (dot(mix_t[:, :NODES], grad_before) + dot(mix_t[:, NODES:], grad_before)).astype(BF16)
        parts = (
            (unit_t, lambda: gm_s[...]),
            (unit_t, lambda: gb_s[at]),
            (act_t, lambda: up[at + 1]),
        )
        for n, (left, right) in enumerate(parts):
            rows = pl.ds(n * features, features)
            product = dot(left[i], right())

            @pl.when(t == 0)
            def _():
                acc[rows, :] = product

            @pl.when(t > 0)
            def _():
                acc[rows, :] += product

        @pl.when(t == 0)
        def _():
            gacc[...] = gp_s[at]

        @pl.when(t > 0)
        def _():
            gacc[...] += gp_s[at]

    def finish_sends():
        for k in (1, 2, 3):
            give_gain(k).wait_send()
            for i in range(3):
                give(k, i).wait_send()
                share(k, i).wait_send()

        @pl.when(busy)
        def _():
            for c in range(CHUNKS):

                @pl.when(early)
                def _():
                    hop_f(c).wait_send()

                @pl.when(late)
                def _():
                    hop_b(c).wait_send()

            @pl.loop(0, LAYERS)
            def _(l):
                @pl.when(l != m)
                def _():
                    for i in range(5):
                        hand_in(l, i).wait_send()

    if not SUM:
        finish_sends()
        return

    half = acc.shape[0] // CORES
    chunk = half // RING
    piece = chunk // 2

    def toward(d):
        return dp_at(yh, z_next if d == 0 else z_prev, core)

    def owner_at(d, shift):
        return lax.rem(z + (shift if d == 0 else RING - shift), RING)

    def rows_at(c, u, owner):
        return pl.ds(pl.multiple_of(c * half + owner * chunk + u * piece, 16), piece)

    def steps(u, d):
        return FAR if u == d else FAR - 1

    flows = [(u, d) for long in (True, False) for u in range(2) for d in range(2) if (u == d) == long]

    quarter = half // 4

    def quarter_rows(c, i):
        return pl.ds(pl.multiple_of(c * half + i * quarter, 16), quarter)

    def to_sib(i):
        return remote(acc.at[quarter_rows(1 - core, i)], sib_buf.at[i], sib_send.at[i], sib_recv.at[i], sibling)

    g_to_sib = remote(gacc, g_sib, gs_sem.at[0], gs_sem.at[1], sibling)
    for i in range(4):
        to_sib(i).start()
    g_to_sib.start()

    def rs(u, d, t):
        rows = rows_at(core, u, owner_at(d, steps(u, d) - t))
        return remote(acc.at[rows], ring_buf.at[u, d, t], rs_send.at[u, d, t], rs_recv.at[u, d, t], toward(d))

    def take(u, d, t):
        rs(u, d, t).wait_recv()
        acc[rows_at(core, u, owner_at(d, steps(u, d) - t - 1)), :] += ring_buf[u, d, t]

    for i in range(4):
        to_sib(i).wait()
        acc[quarter_rows(core, i), :] += sib_buf[i]
    for u, d in flows:
        rs(u, d, 0).start()
    g_to_sib.wait()
    gacc[...] += g_sib[...]
    g_to_y = remote(gacc, g_y, gy_sem.at[0], gy_sem.at[1], across)
    g_to_y.start()
    for t in range(1, FAR):
        for u, d in flows:
            if t < steps(u, d):
                take(u, d, t - 1)
                rs(u, d, t).start()

    def y_copy(u):
        return remote(acc.at[rows_at(core, u, z)], y_buf.at[u], y_send.at[u], y_recv.at[u], across)

    for u in range(2):
        for d in (1 - u, u):
            take(u, d, steps(u, d) - 1)
        y_copy(u).start()

    g_to_y.wait()
    g_z[z] = gacc[...] + g_y[...]

    def g_spread(d):
        return remote(g_z.at[z], g_z.at[z], gz_send.at[d - 1], gz_recv.at[d - 1], dp_at(yh, lax.rem(z + d, RING), core))

    def g_arrive(d):
        at = lax.rem(z - d + RING, RING)
        return remote(g_z.at[at], g_z.at[at], gz_send.at[d - 1], gz_recv.at[d - 1], dp_at(yh, at, core))

    for d in range(1, RING):
        g_spread(d).start()

    def spread(u, d, t):
        rows = rows_at(core, u, owner_at(1 - d, t))
        return remote(out.at[rows], out.at[rows], ag_send.at[u, d, t], ag_recv.at[u, d, t], toward(d))

    def arrive(u, d, t):
        rows = rows_at(core, u, owner_at(1 - d, t + 1))
        return remote(out.at[rows], out.at[rows], ag_send.at[u, d, t], ag_recv.at[u, d, t], toward(d))

    def hand_over(u, owner):
        rows = rows_at(core, u, owner)
        return remote(out.at[rows], out.at[rows], fw_send.at[u, owner], fw_recv.at[u, owner], sibling)

    def handed_over(u, owner):
        rows = rows_at(1 - core, u, owner)
        return remote(out.at[rows], out.at[rows], fw_send.at[u, owner], fw_recv.at[u, owner], sibling)

    for u in range(2):
        y_copy(u).wait()
        rows = rows_at(core, u, z)
        out[rows, :] = acc[rows, :] + y_buf[u]
        for d in (u, 1 - u):
            spread(u, d, 0).start()
        hand_over(u, z).start()

    for t in range(FAR):
        for u, d in flows:
            if t < steps(u, d):
                arrive(u, d, t).wait_recv()
                if t + 1 < steps(u, d):
                    spread(u, d, t + 1).start()
                hand_over(u, owner_at(1 - d, t + 1)).start()

    for d in range(1, RING):
        g_arrive(d).wait_recv()
    total = g_z[0]
    for i in range(1, RING):
        total = total + g_z[i]
    gain_out[...] = jnp.broadcast_to(jnp.sum(total, axis=0, keepdims=True), gain_out.shape)

    for u in range(2):
        for i in range(RING):
            handed_over(u, i).wait_recv()
            hand_over(u, i).wait_send()
    for u, d in flows:
        for t in range(steps(u, d)):
            rs(u, d, t).wait_send()
            spread(u, d, t).wait_send()
    for d in range(1, RING):
        g_spread(d).wait_send()
    finish_sends()


def on_device(sections, replicas, *args):
    samples, grid_rows, features = args[0].shape
    loss_scale = 1.0 / math.sqrt(samples * replicas * grid_rows)
    total_rows = 3 * features
    piece = total_rows // CORES // RING // 2
    dma = pltpu.SemaphoreType.DMA
    v = pltpu.VMEM
    tile = (BLOCK, BLOCK)
    vmem_spec = pl.BlockSpec(memory_space=pltpu.VMEM)
    out, gain_out = pl.pallas_call(
        functools.partial(step_kernel, samples, loss_scale),
        out_shape=(
            jax.ShapeDtypeStruct((total_rows, features), F32),
            jax.ShapeDtypeStruct((8, features), F32),
        ),
        in_specs=[pl.BlockSpec(memory_space=pltpu.HBM)] * 12,
        out_specs=(vmem_spec, vmem_spec),
        scratch_shapes=[
            v((grid_rows, features), BF16),
            v((grid_rows, features), BF16),
            v((4,) + tile, BF16),
            v((4,) + tile, BF16),
            v((8,) + tile, BF16),
            pltpu.SMEM((4,), jnp.int32),
            pltpu.SMEM((4,), jnp.int32),
            pltpu.SMEM((8,), jnp.int32),
            v((3, LAYERS, features, features), BF16),
            v((1, features), F32),
            v((LAYERS, 8, features), F32),
            v((NODES, 2 * NODES), BF16),
            v((NODES, 2 * NODES), BF16),
            v((NODES, 2 * grid_rows), BF16),
            v((grid_rows, 2 * NODES), BF16),
            v((NODES, 2 * grid_rows), BF16),
            v((LAYERS + 1, NODES, features), BF16),
            v((LAYERS + 1 + samples, NODES, features), BF16),
            v((LAYERS + samples, NODES, features), BF16),
            v((LAYERS + samples, NODES, features), BF16),
            v((LAYERS + samples, NODES, features), BF16),
            v((LAYERS + samples, 8, features), F32),
            v((LAYERS, NODES, features), F32),
            v((LAYERS, NODES, features), F32),
            v((LAYERS, NODES, 128), F32),
            v((NODES, features), BF16),
            v((NODES, features), F32),
            v((NODES, features), BF16),
            v((samples, features, NODES), BF16),
            v((samples, features, NODES), BF16),
            v((total_rows, features), F32),
            v((8, features), F32),
            v((4, total_rows // CORES // 4, features), F32),
            v((2, 2, FAR, piece, features), F32),
            v((2, piece, features), F32),
            v((8, features), F32),
            v((8, features), F32),
            v((RING, 8, features), F32),
            dma((10,)),
            dma((2,)),
            dma((3, 3)),
            dma((3, 3)),
            dma((3, 3)),
            dma((3, 3)),
            dma((3,)),
            dma((3,)),
            dma((2, CHUNKS)),
            dma((2, CHUNKS)),
            dma((LAYERS, 5)),
            dma((samples, 5)),
            dma((4,)),
            dma((4,)),
            dma((2, 2, FAR)),
            dma((2, 2, FAR)),
            dma((2,)),
            dma((2,)),
            dma((2, 2, FAR)),
            dma((2, 2, FAR)),
            dma((2, RING)),
            dma((2, RING)),
            dma((2,)),
            dma((2,)),
            dma((STEPS,)),
            dma((STEPS,)),
        ],
        compiler_params=pltpu.CompilerParams(
            collective_id=0, has_side_effects=True, vmem_limit_bytes=64 * 1024 * 1024 - 4096
        ),
        name="train_step",
    )(*args)
    return out.reshape(1, 3, features, features), gain_out[:1]


def solution(mesh):
    placed = (
        P("dp", None, None),
        P("dp", None, None),
        P(),
        P(),
        P(),
        P(),
        P(),
        P(),
        P("section", None, None),
        P("section", None, None),
        P("section", None, None),
        P("section", None),
    )
    return jax.shard_map(
        functools.partial(on_device, mesh.shape["section"], mesh.shape["dp"]),
        mesh=mesh,
        in_specs=placed,
        out_specs=(P("section", None, None, None), P("section", None)),
        check_vma=False,
    )
```

time: 214 us -> 163 us (0.76)
  Pallas kernels: 201 us -> 157 us
  local copies, waits for them, and re-layouts: 10.5 us -> 5.15 us
    pallas_call x1, Pallas kernels: 201 us -> 157 us  [on_device(): pl.pallas_call(functools.partial(step_kernel, samples, loss_scale), out_s...]
    unnamed x22 -> x1, local copies, waits for them, and re-layouts: 9.93 us -> 3.86 us
where the time goes in v2:
time: 163 us
  Pallas kernels  157 us (96%)
  local copies, waits for them, and re-layouts  5.15 us (3%)
    pallas_call x1, Pallas kernels, on_device(): pl.pallas_call(functools.partial(step_kernel, samples, loss_scale), out_s...  157 us
    unnamed x1, local copies, waits for them, and re-layouts  3.86 us

profile of v2, /device:TPU:1, one launch (start us, length us, event | category | flops | bytes accessed | tf_op | source)
XLA Modules:
  0.0 162.8 jit_solution(11404512451834309595)
XLA Ops:
  0.6 157.0 %train_step.1 = (f32[1536,512]{1,0:T(8,128)}, f32[8,512]{1,0:T(8,128)}) custom-call(bf16[3,512,512]{2,1,0:T(8,128)(2,1)} %lat_hbm.1, bf16[3,512,512]{2,1,0:T(8,128)(2,1)} %tgt_hbm.1, bf16[4,128,128]{2,1,0:T(8,128)(2,1)} %g2m_hbm.1, s32[4]{0:T(128)} %g2m_c_hbm.1, bf16[4,128,128]{2,1,0:T(8,128)(2,1)} %m2m_hbm.1, s32[4]{0:T(128)} %m2m_c_hbm.1, ...), custom_call_target="tpu_custom_call" | custom-call | tf_op jit(solution)/shard_map/train_step/pallas_call | solution.py:671
  157.6 1.3 slice.3
  158.9 3.9 %copy.15 = f32[1,3,512,512]{3,2,1,0:T(8,128)} copy(f32[1,3,512,512]{3,2,1,0:T(8,128)} %bitcast.1) | data formatting | bytes 6291456

commit v3 on v2

--- a/solution.py
+++ b/solution.py
@@ -69,15 +69,12 @@
     unit_s,
     act_s,
     gb_s,
-    gp_s,
     slope_s,
     normed_s,
     inv_s,
     msg_s,
     up_s,
     gm_s,
-    unit_t,
-    act_t,
     acc,
     gacc,
     sib_buf,
@@ -226,9 +223,8 @@
         return remote(here, here, gn_send.at[k - 1], gn_recv.at[k - 1], sibling)
 
     pl.semaphore_wait(barrier, met)
-    for i in range(3):
-        for k in (1, 2):
-            give(k, i).start()
+    give(1, 0).start()
+    give(2, 0).start()
     for load in loads:
         load.wait()
     gains[m] = jnp.broadcast_to(gain_v[...], (8, features))
@@ -268,6 +264,12 @@
                 kept = kept_if(m2g_c[t], b, tile_t)
                 seed_t[b * BLOCK : (b + 1) * BLOCK, (4 * k + r) * BLOCK : (4 * k + r + 1) * BLOCK] = kept
 
+    give(1, 0).wait_send()
+    give(1, 1).start()
+    give(1, 2).start()
+    give(2, 0).wait_send()
+    give(2, 1).start()
+
     span = NODES // CHUNKS
 
     def rows_of(c):
@@ -279,118 +281,103 @@
     def hop_b(c):
         return remote(up.at[0, rows_of(c)], up.at[LAYERS, rows_of(c)], hop_send.at[1, c], hop_recv.at[1, c], hop_to)
 
-    kinds = ((unit_s, 0), (act_s, 0), (up, 1), (gb_s, 0), (gp_s, 0))
-
-    def hand_in(layer, i):
-        ref, shift = kinds[i]
+    def hand_in(layer, kind):
+        ref, at = ((h, layer), (up, layer + 1))[kind]
         return remote(
-            ref.at[layer + shift], ref.at[LAYERS + shift + j], pass_send.at[layer, i], pass_recv.at[j, i], member_at(layer)
+            ref.at[at], ref.at[LAYERS + 1 + j], pass_send.at[layer, kind], pass_recv.at[j, kind], member_at(layer)
         )
 
-    def handed_in(from_j, i):
-        ref, shift = kinds[i]
-        here = ref.at[LAYERS + shift + from_j]
-        return remote(here, here, pass_send.at[0, i], pass_recv.at[from_j, i], sibling)
-
-    def forward(l):
-        @pl.when(early & (l == 0))
-        def _():
-            grid_rows = lat.shape[0]
-            h[0] = (dot(enc[:, :grid_rows], lat[...]) + dot(enc[:, grid_rows:], lat[...])).astype(BF16)
-
-        gain = gains[l, 0:1, :]
+    def handed_in(i, kind):
+        here = (h, up)[kind].at[LAYERS + 1 + i]
+        return remote(here, here, pass_send.at[0, kind], pass_recv.at[i, kind], sibling)
+
+    def forward(q, layer, own):
+        at = q if own else q + 1
+        gain = gains[layer, 0:1, :]
         for c in range(CHUNKS):
             rows = rows_of(c)
-
-            @pl.when(late & (l == 0))
-            def _():
-                hop_f(c).wait_recv()
-
-            x = h[l, rows, :].astype(F32)
+            if own:
+
+                @pl.when(late & (q == 0))
+                def _():
+                    hop_f(c).wait_recv()
+
+            x = h[at, rows, :].astype(F32)
             center = x - jnp.mean(x, axis=-1, keepdims=True)
             inverse = lax.rsqrt(jnp.mean(center * center, axis=-1, keepdims=True) + EPSILON)
             normed = center * inverse
             unit = (normed * gain).astype(BF16)
-            normed_s[l, rows, :] = normed
-            inv_s[l, rows, :] = jnp.broadcast_to(inverse, (span, 128))
-            unit_s[l, rows, :] = unit
-            msg_s[rows, :] = dot(unit, w[0, l]).astype(BF16)
-            up_s[rows, :] = dot(unit, w[1, l])
+            normed_s[q, rows, :] = normed
+            if own:
+                inv_s[q, rows, :] = jnp.broadcast_to(inverse, (span, 128))
+            unit_s[q, rows, :] = unit
+            msg_s[rows, :] = dot(unit, w[0, layer]).astype(BF16)
+            up_s[rows, :] = dot(unit, w[1, layer])
         for c in range(CHUNKS):
             rows = rows_of(c)
             before = up_s[rows, :] + dot(mix[rows, :NODES], msg_s[...]) + dot(mix[rows, NODES:], msg_s[...])
             sigma = 1.0 / (1.0 + jnp.exp(-before))
             active = (before * sigma).astype(BF16)
-            slope_s[l, rows, :] = sigma * (1.0 + before * (1.0 - sigma))
-            act_s[l, rows, :] = active
-            output = h[l, rows, :].astype(F32) + dot(active, w[2, l])
-            h[l + 1, rows, :] = output.astype(BF16)
-
-            @pl.when(early & (l == LAYERS - 1))
+            slope_s[q, rows, :] = sigma * (1.0 + before * (1.0 - sigma))
+            act_s[q, rows, :] = active
+            if own:
+                output = h[q, rows, :].astype(F32) + dot(active, w[2, layer])
+                h[q + 1, rows, :] = output.astype(BF16)
+
+                @pl.when(early & (q == LAYERS - 1))
+                def _():
+                    hop_f(c).start()
+
+    def encode():
+        grid_rows = lat.shape[0]
+        h[0] = (dot(enc[:, :grid_rows], lat[...]) + dot(enc[:, grid_rows:], lat[...])).astype(BF16)
+
+    def decode():
+        upstream = jnp.zeros((NODES, features), F32)
+        for r in range(4):
+            here = pl.ds(r * BLOCK, BLOCK)
+            predicted = dot(pred[here, :NODES], h[LAYERS]) + dot(pred[here, NODES:], h[LAYERS])
+            target = tgt[r * BLOCK : (r + 1) * BLOCK, :].astype(F32)
+            residual = ((predicted - target) * loss_scale).astype(BF16)
+            for k in range(2):
+                part = seed_t[:, (4 * k + r) * BLOCK : (4 * k + r + 1) * BLOCK]
+                upstream = upstream + dot(part, residual)
+        up[LAYERS] = upstream.astype(BF16)
+
+    def backward(q, layer, own):
+        gain = gains[layer, 0:1, :]
+        gb_s[q] = (dot_nt(up[q + 1], w[2, layer]) * slope_s[q]).astype(BF16)
+        gm_s[q] = (dot(mix_t[:, :NODES], gb_s[q]) + dot(mix_t[:, NODES:], gb_s[q])).astype(BF16)
+        up_s[...] = dot_nt(gb_s[q], w[1, layer]) + dot_nt(gm_s[q], w[0, layer])
+
+        @pl.when(layer == m)
+        def _():
+            gacc[...] += jnp.sum((up_s[...] * normed_s[q]).reshape(NODES // 8, 8, features), axis=0)
+
+        if own:
+
+            @pl.when(late | (q > 0))
             def _():
-                hop_f(c).start()
-
-        @pl.when(l != m)
-        def _():
-            hand_in(l, 0).start()
-            hand_in(l, 1).start()
-
-        @pl.when(late & (l == LAYERS - 1))
-        def _():
-            upstream = jnp.zeros((NODES, features), F32)
-            for r in range(4):
-                here = pl.ds(r * BLOCK, BLOCK)
-                predicted = dot(pred[here, :NODES], h[LAYERS]) + dot(pred[here, NODES:], h[LAYERS])
-                target = tgt[r * BLOCK : (r + 1) * BLOCK, :].astype(F32)
-                residual = ((predicted - target) * loss_scale).astype(BF16)
-                for k in range(2):
-                    part = seed_t[:, (4 * k + r) * BLOCK : (4 * k + r + 1) * BLOCK]
-                    upstream = upstream + dot(part, residual)
-            up[LAYERS] = upstream.astype(BF16)
-
-    def backward(l):
-        gain = gains[l, 0:1, :]
-        for c in range(CHUNKS):
-            rows = rows_of(c)
-
-            @pl.when(early & (l == LAYERS - 1))
-            def _():
-                hop_b(c).wait_recv()
-
-            grad_active = dot_nt(up[l + 1, rows, :], w[2, l])
-            gb_s[l, rows, :] = (grad_active * slope_s[l, rows, :]).astype(BF16)
-
-        @pl.when(l != m)
-        def _():
-            hand_in(l, 2).start()
-            hand_in(l, 3).start()
-
-        gm_s[...] = (dot(mix_t[:, :NODES], gb_s[l]) + dot(mix_t[:, NODES:], gb_s[l])).astype(BF16)
-        for c in range(CHUNKS):
-            rows = rows_of(c)
-            grad_unit = dot_nt(gb_s[l, rows, :], w[1, l]) + dot_nt(gm_s[rows, :], w[0, l])
-            normed = normed_s[l, rows, :]
-            part = jnp.sum((grad_unit * normed).reshape(span // 8, 8, features), axis=0)
-            gp_s[l] = part if c == 0 else gp_s[l] + part
-
-            @pl.when(late | (l > 0))
-            def _():
-                grad_normed = grad_unit * gain
-                inverse = inv_s[l, rows, :][:, :1]
-                grad_inputs = up[l + 1, rows, :].astype(F32) + inverse * (
-                    grad_normed
-                    - jnp.mean(grad_normed, axis=-1, keepdims=True)
-                    - normed * jnp.mean(grad_normed * normed, axis=-1, keepdims=True)
-                )
-                up[l, rows, :] = grad_inputs.astype(BF16)
-
-            @pl.when(late & (l == 0))
-            def _():
-                hop_b(c).start()
-
-        @pl.when(l != m)
-        def _():
-            hand_in(l, 4).start()
+                for c in range(CHUNKS):
+                    rows = rows_of(c)
+                    grad_normed = up_s[rows, :] * gain
+                    normed = normed_s[q, rows, :]
+                    inverse = inv_s[q, rows, :][:, :1]
+                    grad_inputs = up[q + 1, rows, :].astype(F32) + inverse * (
+                        grad_normed
+                        - jnp.mean(grad_normed, axis=-1, keepdims=True)
+                        - normed * jnp.mean(grad_normed * normed, axis=-1, keepdims=True)
+                    )
+                    up[q, rows, :] = grad_inputs.astype(BF16)
+
+                    @pl.when(late & (q == 0))
+                    def _():
+                        hop_b(c).start()
+
+    def add_weight_grads(q):
+        for n, (left, right) in enumerate(((unit_s, gm_s), (unit_s, gb_s), (act_s, None))):
+            rows = pl.ds(n * features, features)
+            acc[rows, :] += dot(left[q].T, up[q + 1] if right is None else right[q])
 
     def round_of(l):
         last = 0
@@ -407,11 +394,13 @@
         def _():
             for k in (1, 2, 3):
                 got_gain(k).wait_recv()
-            for k, i in ((1, 0), (1, 1), (2, 0), (1, 2)):
+            for k, i in ((1, 0), (2, 0), (1, 1), (1, 2)):
                 got(k, i).wait_recv()
                 if k == 2:
                     give(3, i).start()
                 share(k, i).start()
+            give(2, 1).wait_send()
+            give(2, 2).start()
             for i in range(3):
                 shared(1, i).wait_recv()
 
@@ -434,35 +423,67 @@
 
         @pl.when(busy & (round_of(l) == e))
         def _():
-            forward(l)
-
-    def turn():
-        @pl.loop(0, samples)
-        def _(i):
-            mine = i == j
-
-            @pl.when(jnp.logical_not(mine))
+            @pl.when(early & (l == 0))
             def _():
-                handed_in(i, 0).wait_recv()
-                handed_in(i, 1).wait_recv()
-
-            at = jnp.where(mine, m, LAYERS + i)
-            unit_t[i] = unit_s[at].T
-            act_t[i] = act_s[at].T
-
-    @pl.when(early)
+                encode()
+
+            @pl.when(late & (l != m))
+            def _():
+                @pl.when(l > 0)
+                def _():
+                    hand_in(l, 0).start()
+
+            forward(l, l, True)
+
+    @pl.when(busy & late)
     def _():
-        turn()
-
-    @pl.loop(0, LAYERS)
+        decode()
+
+    @pl.when(busy)
+    def _():
+        @pl.loop(0, LAYERS)
+        def _(l):
+            @pl.when((l != m) & (early | (l == 0)))
+            def _():
+                hand_in(l, 0).start()
+
+        @pl.when(m != LAYERS - 1)
+        def _():
+            @pl.when(late)
+            def _():
+                hand_in(LAYERS - 1, 1).start()
+
+    acc[...] = jnp.zeros_like(acc)
+    gacc[...] = jnp.zeros_like(gacc)
+
+    @pl.loop(0, LAYERS + samples)
     def _(t):
-        @pl.when(busy)
-        def _():
-            backward(LAYERS - 1 - t)
-
-    @pl.when(late)
-    def _():
-        turn()
+        other = jnp.where(early, t, t - LAYERS)
+        l = LAYERS - 1 - jnp.where(early, t - samples, t)
+
+        @pl.when((other >= 0) & (other < samples) & (other != j))
+        def _():
+            handed_in(other, 0).wait_recv()
+            forward(LAYERS + other, m, False)
+
+        @pl.when(busy & (l >= 0) & (l < LAYERS))
+        def _():
+            @pl.when(early & (l == LAYERS - 1))
+            def _():
+                for c in range(CHUNKS):
+                    hop_b(c).wait_recv()
+
+                @pl.when(m != LAYERS - 1)
+                def _():
+                    hand_in(LAYERS - 1, 1).start()
+
+            @pl.when(late | (l > 0) | (m == 0))
+            def _():
+                backward(l, l, True)
+
+            @pl.when((l > 0) & (l - 1 != m))
+            def _():
+                hand_in(l - 1, 1).start()
 
     @pl.loop(0, samples)
     def _(t):
@@ -471,42 +492,17 @@
 
         @pl.when(jnp.logical_not(mine))
         def _():
-            for kind in (2, 3, 4):
-                handed_in(i, kind).wait_recv()
-
-        at = jnp.where(mine, m, LAYERS + i)
-        grad_before = gb_s[at]
-        gm_s[...] = (dot(mix_t[:, :NODES], grad_before) + dot(mix_t[:, NODES:], grad_before)).astype(BF16)
-        parts = (
-            (unit_t, lambda: gm_s[...]),
-            (unit_t, lambda: gb_s[at]),
-            (act_t, lambda: up[at + 1]),
-        )
-        for n, (left, right) in enumerate(parts):
-            rows = pl.ds(n * features, features)
-            product = dot(left[i], right())
-
-            @pl.when(t == 0)
-            def _():
-                acc[rows, :] = product
-
-            @pl.when(t > 0)
-            def _():
-                acc[rows, :] += product
-
-        @pl.when(t == 0)
-        def _():
-            gacc[...] = gp_s[at]
-
-        @pl.when(t > 0)
-        def _():
-            gacc[...] += gp_s[at]
+            handed_in(i, 1).wait_recv()
+            backward(LAYERS + i, m, False)
+
+        add_weight_grads(jnp.where(mine, m, LAYERS + i))
 
     def finish_sends():
         for k in (1, 2, 3):
             give_gain(k).wait_send()
             for i in range(3):
-                give(k, i).wait_send()
+                if (k, i) not in ((1, 0), (2, 0), (2, 1)):
+                    give(k, i).wait_send()
                 share(k, i).wait_send()
 
         @pl.when(busy)
@@ -525,8 +521,8 @@
             def _(l):
                 @pl.when(l != m)
                 def _():
-                    for i in range(5):
-                        hand_in(l, i).wait_send()
+                    for kind in range(2):
+                        hand_in(l, kind).wait_send()
 
     if not SUM:
         finish_sends()
@@ -644,7 +640,7 @@
     total = g_z[0]
     for i in range(1, RING):
         total = total + g_z[i]
-    gain_out[...] = jnp.broadcast_to(jnp.sum(total, axis=0, keepdims=True), gain_out.shape)
+    gain_out[...] = jnp.sum(total, axis=0, keepdims=True)
 
     for u in range(2):
         for i in range(RING):
@@ -672,7 +668,7 @@
         functools.partial(step_kernel, samples, loss_scale),
         out_shape=(
             jax.ShapeDtypeStruct((total_rows, features), F32),
-            jax.ShapeDtypeStruct((8, features), F32),
+            jax.ShapeDtypeStruct((1, features), F32),
         ),
         in_specs=[pl.BlockSpec(memory_space=pltpu.HBM)] * 12,
         out_specs=(vmem_spec, vmem_spec),
@@ -693,20 +689,17 @@
             v((NODES, 2 * grid_rows), BF16),
             v((grid_rows, 2 * NODES), BF16),
             v((NODES, 2 * grid_rows), BF16),
-            v((LAYERS + 1, NODES, features), BF16),
+            v((LAYERS + 1 + samples, NODES, features), BF16),
             v((LAYERS + 1 + samples, NODES, features), BF16),
             v((LAYERS + samples, NODES, features), BF16),
             v((LAYERS + samples, NODES, features), BF16),
             v((LAYERS + samples, NODES, features), BF16),
-            v((LAYERS + samples, 8, features), F32),
-            v((LAYERS, NODES, features), F32),
-            v((LAYERS, NODES, features), F32),
+            v((LAYERS + samples, NODES, features), F32),
+            v((LAYERS + samples, NODES, features), F32),
             v((LAYERS, NODES, 128), F32),
             v((NODES, features), BF16),
             v((NODES, features), F32),
-            v((NODES, features), BF16),
-            v((samples, features, NODES), BF16),
-            v((samples, features, NODES), BF16),
+            v((LAYERS + samples, NODES, features), BF16),
             v((total_rows, features), F32),
             v((8, features), F32),
             v((4, total_rows // CORES // 4, features), F32),
@@ -725,8 +718,8 @@
             dma((3,)),
             dma((2, CHUNKS)),
             dma((2, CHUNKS)),
-            dma((LAYERS, 5)),
-            dma((samples, 5)),
+            dma((LAYERS, 2)),
+            dma((samples, 2)),
             dma((4,)),
             dma((4,)),
             dma((2, 2, FAR)),
@@ -743,11 +736,11 @@
             dma((STEPS,)),
         ],
         compiler_params=pltpu.CompilerParams(
-            collective_id=0, has_side_effects=True, vmem_limit_bytes=64 * 1024 * 1024 - 4096
+            collective_id=0, has_side_effects=True, vmem_limit_bytes=44 * 1024 * 1024
         ),
         name="train_step",
-    )(*args)
-    return out.reshape(1, 3, features, features), gain_out[:1]
+    )(*[pltpu.with_memory_space_constraint(a, pltpu.HBM) for a in args])
+    return out.reshape(1, 3, features, features), gain_out
 
 
 def solution(mesh):

time: 163 us -> 137 us (0.84)
  Pallas kernels: 157 us -> 134 us
  local copies, waits for them, and re-layouts: 5.15 us -> 2.24 us
    pallas_call x1, Pallas kernels: 157 us -> 134 us  [on_device(): pl.pallas_call(functools.partial(step_kernel, samples, loss_scale), out_s...]
    unnamed x1 -> x2, local copies, waits for them, and re-layouts: 3.86 us -> 2.24 us
where the time goes in v3:
time: 137 us
  Pallas kernels  134 us (98%)
  local copies, waits for them, and re-layouts  2.24 us (2%)
    pallas_call x1, Pallas kernels, on_device(): pl.pallas_call(functools.partial(step_kernel, samples, loss_scale), out_s...  134 us

profile of v3, /device:TPU:1, one launch (start us, length us, event | category | flops | bytes accessed | tf_op | source)
XLA Modules:
  0.0 137.2 jit_solution(16786844241801889238)
XLA Ops:
  0.6 134.4 %train_step.1 = (f32[1536,512]{1,0:T(8,128)S(1)}, f32[1,512]{1,0:T(1,128)S(1)}) custom-call(bf16[3,512,512]{2,1,0:T(8,128)(2,1)} %lat_hbm.1, bf16[3,512,512]{2,1,0:T(8,128)(2,1)} %tgt_hbm.1, bf16[4,128,128]{2,1,0:T(8,128)(2,1)} %g2m_hbm.1, s32[4]{0:T(128)} %g2m_c_hbm.1, bf16[4,128,128]{2,1,0:T(8,128)(2,1)} %m2m_hbm.1, s32[4]{0:T(128)} %m2m_c_hbm.1, ...), custom_call_target="tpu_custom_call" | custom-call | tf_op jit(solution)/shard_map/train_step/pallas_call | solution.py:667
  135.0 1.7 %copy.16 = f32[1,3,512,512]{3,2,1,0:T(8,128)} copy(f32[1,3,512,512]{3,2,1,0:T(8,128)S(1)} %bitcast.1) | data formatting | bytes 6291456
  136.7 0.6 copy.17

commit v4 on v3

--- a/solution.py
+++ b/solution.py
@@ -20,6 +20,7 @@
 RING = 8
 STEPS = RING - 1
 FAR = RING // 2
+STREAMS = 4
 SUM = True
 
 
@@ -294,14 +295,15 @@
     def forward(q, layer, own):
         at = q if own else q + 1
         gain = gains[layer, 0:1, :]
+        if own:
+
+            @pl.when(late & (q == 0))
+            def _():
+                for c in range(CHUNKS):
+                    hop_f(c).wait_recv()
+
         for c in range(CHUNKS):
             rows = rows_of(c)
-            if own:
-
-                @pl.when(late & (q == 0))
-                def _():
-                    hop_f(c).wait_recv()
-
             x = h[at, rows, :].astype(F32)
             center = x - jnp.mean(x, axis=-1, keepdims=True)
             inverse = lax.rsqrt(jnp.mean(center * center, axis=-1, keepdims=True) + EPSILON)
@@ -323,9 +325,11 @@
             if own:
                 output = h[q, rows, :].astype(F32) + dot(active, w[2, layer])
                 h[q + 1, rows, :] = output.astype(BF16)
-
-                @pl.when(early & (q == LAYERS - 1))
-                def _():
+        if own:
+
+            @pl.when(early & (q == LAYERS - 1))
+            def _():
+                for c in range(CHUNKS):
                     hop_f(c).start()
 
     def encode():
@@ -370,9 +374,10 @@
                     )
                     up[q, rows, :] = grad_inputs.astype(BF16)
 
-                    @pl.when(late & (q == 0))
-                    def _():
-                        hop_b(c).start()
+            @pl.when(late & (q == 0))
+            def _():
+                for c in range(CHUNKS):
+                    hop_b(c).start()
 
     def add_weight_grads(q):
         for n, (left, right) in enumerate(((unit_s, gm_s), (unit_s, gb_s), (act_s, None))):
@@ -530,7 +535,7 @@
 
     half = acc.shape[0] // CORES
     chunk = half // RING
-    piece = chunk // 2
+    piece = chunk // STREAMS
 
     def toward(d):
         return dp_at(yh, z_next if d == 0 else z_prev, core)
@@ -539,24 +544,29 @@
         return lax.rem(z + (shift if d == 0 else RING - shift), RING)
 
     def rows_at(c, u, owner):
-        return pl.ds(pl.multiple_of(c * half + owner * chunk + u * piece, 16), piece)
+        return pl.ds(pl.multiple_of(c * half + owner * chunk + u * piece, 8), piece)
 
     def steps(u, d):
-        return FAR if u == d else FAR - 1
-
-    flows = [(u, d) for long in (True, False) for u in range(2) for d in range(2) if (u == d) == long]
-
-    quarter = half // 4
-
-    def quarter_rows(c, i):
-        return pl.ds(pl.multiple_of(c * half + i * quarter, 16), quarter)
-
-    def to_sib(i):
-        return remote(acc.at[quarter_rows(1 - core, i)], sib_buf.at[i], sib_send.at[i], sib_recv.at[i], sibling)
+        return FAR if u % 2 == d else FAR - 1
+
+    pairs = [((u, 0), (u + 1, 1)) for u in range(0, STREAMS, 2)] + [((u + 1, 0), (u, 1)) for u in range(0, STREAMS, 2)]
+    flows = [flow for pair in pairs for flow in pair]
+
+    def chunk_rows(c, shift):
+        return pl.ds(pl.multiple_of(c * half + lax.rem(z + shift, RING) * chunk, 8), chunk)
+
+    def to_sib(shift):
+        rows = chunk_rows(1 - core, shift)
+        return remote(acc.at[rows], sib_buf.at[shift], sib_send.at[shift], sib_recv.at[shift], sibling)
+
+    def from_sib(*shifts):
+        for shift in shifts:
+            to_sib(shift).wait_recv()
+            acc[chunk_rows(core, shift), :] += sib_buf[shift]
 
     g_to_sib = remote(gacc, g_sib, gs_sem.at[0], gs_sem.at[1], sibling)
-    for i in range(4):
-        to_sib(i).start()
+    for shift in (4, 3, 5, 2, 6, 1, 7, 0):
+        to_sib(shift).start()
     g_to_sib.start()
 
     def rs(u, d, t):
@@ -567,11 +577,22 @@
         rs(u, d, t).wait_recv()
         acc[rows_at(core, u, owner_at(d, steps(u, d) - t - 1)), :] += ring_buf[u, d, t]
 
-    for i in range(4):
-        to_sib(i).wait()
-        acc[quarter_rows(core, i), :] += sib_buf[i]
-    for u, d in flows:
-        rs(u, d, 0).start()
+    def start_pair(n):
+        if n > 0:
+            for u, d in pairs[n - 1]:
+                rs(u, d, 0).wait_send()
+        for u, d in pairs[n]:
+            rs(u, d, 0).start()
+
+    from_sib(4)
+    start_pair(0)
+    from_sib(3, 5)
+    start_pair(1)
+    from_sib(2, 6)
+    start_pair(2)
+    from_sib(1, 7)
+    start_pair(3)
+    from_sib(0)
     g_to_sib.wait()
     gacc[...] += g_sib[...]
     g_to_y = remote(gacc, g_y, gy_sem.at[0], gy_sem.at[1], across)
@@ -585,8 +606,8 @@
     def y_copy(u):
         return remote(acc.at[rows_at(core, u, z)], y_buf.at[u], y_send.at[u], y_recv.at[u], across)
 
-    for u in range(2):
-        for d in (1 - u, u):
+    for u in range(STREAMS):
+        for d in (1 - u % 2, u % 2):
             take(u, d, steps(u, d) - 1)
         y_copy(u).start()
 
@@ -619,11 +640,11 @@
         rows = rows_at(1 - core, u, owner)
         return remote(out.at[rows], out.at[rows], fw_send.at[u, owner], fw_recv.at[u, owner], sibling)
 
-    for u in range(2):
+    for u in range(STREAMS):
         y_copy(u).wait()
         rows = rows_at(core, u, z)
         out[rows, :] = acc[rows, :] + y_buf[u]
-        for d in (u, 1 - u):
+        for d in (u % 2, 1 - u % 2):
             spread(u, d, 0).start()
         hand_over(u, z).start()
 
@@ -642,13 +663,16 @@
         total = total + g_z[i]
     gain_out[...] = jnp.sum(total, axis=0, keepdims=True)
 
-    for u in range(2):
+    for shift in range(RING):
+        to_sib(shift).wait_send()
+    for u in range(STREAMS):
         for i in range(RING):
             handed_over(u, i).wait_recv()
             hand_over(u, i).wait_send()
     for u, d in flows:
         for t in range(steps(u, d)):
-            rs(u, d, t).wait_send()
+            if t > 0 or (u, d) in pairs[-1]:
+                rs(u, d, t).wait_send()
             spread(u, d, t).wait_send()
     for d in range(1, RING):
         g_spread(d).wait_send()
@@ -659,7 +683,8 @@
     samples, grid_rows, features = args[0].shape
     loss_scale = 1.0 / math.sqrt(samples * replicas * grid_rows)
     total_rows = 3 * features
-    piece = total_rows // CORES // RING // 2
+    chunk = total_rows // CORES // RING
+    piece = chunk // STREAMS
     dma = pltpu.SemaphoreType.DMA
     v = pltpu.VMEM
     tile = (BLOCK, BLOCK)
@@ -702,9 +727,9 @@
             v((LAYERS + samples, NODES, features), BF16),
             v((total_rows, features), F32),
             v((8, features), F32),
-            v((4, total_rows // CORES // 4, features), F32),
-            v((2, 2, FAR, piece, features), F32),
-            v((2, piece, features), F32),
+            v((RING, chunk, features), F32),
+            v((STREAMS, 2, FAR, piece, features), F32),
+            v((STREAMS, piece, features), F32),
             v((8, features), F32),
             v((8, features), F32),
             v((RING, 8, features), F32),
@@ -720,16 +745,16 @@
             dma((2, CHUNKS)),
             dma((LAYERS, 2)),
             dma((samples, 2)),
-            dma((4,)),
-            dma((4,)),
-            dma((2, 2, FAR)),
-            dma((2, 2, FAR)),
-            dma((2,)),
-            dma((2,)),
-            dma((2, 2, FAR)),
-            dma((2, 2, FAR)),
-            dma((2, RING)),
-            dma((2, RING)),
+            dma((RING,)),
+            dma((RING,)),
+            dma((STREAMS, 2, FAR)),
+            dma((STREAMS, 2, FAR)),
+            dma((STREAMS,)),
+            dma((STREAMS,)),
+            dma((STREAMS, 2, FAR)),
+            dma((STREAMS, 2, FAR)),
+            dma((STREAMS, RING)),
+            dma((STREAMS, RING)),
             dma((2,)),
             dma((2,)),
             dma((STEPS,)),

time: 137 us -> 131 us (0.956)
  Pallas kernels: 134 us -> 128 us
    pallas_call x1, Pallas kernels: 134 us -> 128 us  [on_device(): pl.pallas_call(functools.partial(step_kernel, samples, loss_scale), out_s...]
where the time goes in v4:
time: 131 us
  Pallas kernels  128 us (98%)
  local copies, waits for them, and re-layouts  2.24 us (2%)
    pallas_call x1, Pallas kernels, on_device(): pl.pallas_call(functools.partial(step_kernel, samples, loss_scale), out_s...  128 us

profile of v4, /device:TPU:1, one launch (start us, length us, event | category | flops | bytes accessed | tf_op | source)
XLA Modules:
  0.0 131.3 jit_solution(7161067830453869525)
XLA Ops:
  0.6 128.4 %train_step.1 = (f32[1536,512]{1,0:T(8,128)S(1)}, f32[1,512]{1,0:T(1,128)S(1)}) custom-call(bf16[3,512,512]{2,1,0:T(8,128)(2,1)} %lat_hbm.1, bf16[3,512,512]{2,1,0:T(8,128)(2,1)} %tgt_hbm.1, bf16[4,128,128]{2,1,0:T(8,128)(2,1)} %g2m_hbm.1, s32[4]{0:T(128)} %g2m_c_hbm.1, bf16[4,128,128]{2,1,0:T(8,128)(2,1)} %m2m_hbm.1, s32[4]{0:T(128)} %m2m_c_hbm.1, ...), custom_call_target="tpu_custom_call" | custom-call | tf_op jit(solution)/shard_map/train_step/pallas_call | solution.py:692
  129.0 1.7 %copy.16 = f32[1,3,512,512]{3,2,1,0:T(8,128)} copy(f32[1,3,512,512]{3,2,1,0:T(8,128)S(1)} %bitcast.1) | data formatting | bytes 6291456
  130.7 0.6 copy.17

commit v5 on v4

--- a/solution.py
+++ b/solution.py
@@ -15,6 +15,7 @@
 F32 = jnp.float32
 BF16 = jnp.bfloat16
 CHUNKS = 2
+GUEST = 2
 LAYERS = 4
 CORES = 2
 RING = 8
@@ -94,6 +95,8 @@
     gn_recv,
     hop_send,
     hop_recv,
+    guest_send,
+    guest_recv,
     pass_send,
     pass_recv,
     sib_send,
@@ -124,6 +127,8 @@
     late = stage == 1
     j = jnp.where(early, m, 2 * (1 - mx) + my)
     busy = j < samples
+    host = early & (m == 0)
+    guest = early & (m == 2)
 
     def dp_at(y_, z_, c_):
         return {"dp": (y_ * RING + z_) * CORES + c_}
@@ -183,11 +188,13 @@
         )
     ]
     sample = jnp.minimum(j, samples - 1)
-    lat_load = pltpu.make_async_copy(lat_hbm.at[sample], lat, io_sem.at[0])
+    lat_load = pltpu.make_async_copy(lat_hbm.at[sample], lat.at[0], io_sem.at[0])
+    guest_load = pltpu.make_async_copy(lat_hbm.at[GUEST], lat.at[1], io_sem.at[2])
     tgt_load = pltpu.make_async_copy(tgt_hbm.at[sample], tgt, io_sem.at[1])
     for load in loads:
         load.start()
     lat_load.start()
+    guest_load.start()
     tgt_load.start()
 
     def half_of(i, layer, c):
@@ -244,6 +251,7 @@
                 mix_t[b * BLOCK : (b + 1) * BLOCK, (2 * k + r) * BLOCK : (2 * k + r + 1) * BLOCK] = kept.T
 
     lat_load.wait()
+    guest_load.wait()
     tgt_load.wait()
 
     @pl.when(early)
@@ -292,16 +300,8 @@
         here = (h, up)[kind].at[LAYERS + 1 + i]
         return remote(here, here, pass_send.at[0, kind], pass_recv.at[i, kind], sibling)
 
-    def forward(q, layer, own):
-        at = q if own else q + 1
+    def forward(q, layer, at, output_at=None):
         gain = gains[layer, 0:1, :]
-        if own:
-
-            @pl.when(late & (q == 0))
-            def _():
-                for c in range(CHUNKS):
-                    hop_f(c).wait_recv()
-
         for c in range(CHUNKS):
             rows = rows_of(c)
             x = h[at, rows, :].astype(F32)
@@ -310,8 +310,7 @@
             normed = center * inverse
             unit = (normed * gain).astype(BF16)
             normed_s[q, rows, :] = normed
-            if own:
-                inv_s[q, rows, :] = jnp.broadcast_to(inverse, (span, 128))
+            inv_s[q, rows, :] = jnp.broadcast_to(inverse, (span, 128))
             unit_s[q, rows, :] = unit
             msg_s[rows, :] = dot(unit, w[0, layer]).astype(BF16)
             up_s[rows, :] = dot(unit, w[1, layer])
@@ -322,19 +321,18 @@
             active = (before * sigma).astype(BF16)
             slope_s[q, rows, :] = sigma * (1.0 + before * (1.0 - sigma))
             act_s[q, rows, :] = active
-            if own:
-                output = h[q, rows, :].astype(F32) + dot(active, w[2, layer])
-                h[q + 1, rows, :] = output.astype(BF16)
-        if own:
-
-            @pl.when(early & (q == LAYERS - 1))
-            def _():
-                for c in range(CHUNKS):
-                    hop_f(c).start()
-
-    def encode():
-        grid_rows = lat.shape[0]
-        h[0] = (dot(enc[:, :grid_rows], lat[...]) + dot(enc[:, grid_rows:], lat[...])).astype(BF16)
+            if output_at is not None:
+                output = h[at, rows, :].astype(F32) + dot(active, w[2, layer])
+                h[output_at, rows, :] = output.astype(BF16)
+
+    guest_h = LAYERS + 1 + samples
+
+    def guest_rows(n):
+        return remote(h.at[guest_h + n], h.at[1 + n], guest_send.at[n], guest_recv.at[n], member_at(2))
+
+    def encode(i, at):
+        grid_rows = lat.shape[1]
+        h[at] = (dot(enc[:, :grid_rows], lat[i]) + dot(enc[:, grid_rows:], lat[i])).astype(BF16)
 
     def decode():
         upstream = jnp.zeros((NODES, features), F32)
@@ -389,7 +387,7 @@
         for i in range(LAYERS):
             far = 2 * lax.rem(i // 2 + mx, 2) + lax.rem(i % 2 + my, 2)
             last = jnp.maximum(last, jnp.where(l >= i, far, 0))
-        return jnp.where(early, last, LAYERS - 1)
+        return jnp.where(early, jnp.where(guest, jnp.where(l < 2, LAYERS, 2), last), LAYERS - 1)
 
     @pl.loop(0, LAYERS * LAYERS)
     def _(t):
@@ -426,11 +424,33 @@
             for i in range(3):
                 shared(3, i).wait_recv()
 
+        @pl.when(host & (l == e) & (e < 2))
+        def _():
+            @pl.when(e == 0)
+            def _():
+                encode(1, LAYERS + 1 + GUEST)
+
+            forward(jnp.where(e == 0, LAYERS + GUEST, LAYERS + samples), e, jnp.where(e == 0, LAYERS + 1 + GUEST, guest_h), guest_h + e)
+
+            @pl.when(e == 1)
+            def _():
+                guest_rows(1).start()
+                guest_rows(0).start()
+
         @pl.when(busy & (round_of(l) == e))
         def _():
             @pl.when(early & (l == 0))
             def _():
-                encode()
+                encode(0, 0)
+
+            @pl.when(late & (l == 0))
+            def _():
+                for c in range(CHUNKS):
+                    hop_f(c).wait_recv()
+
+            @pl.when(guest & (l == 2))
+            def _():
+                guest_rows(1).wait_recv()
 
             @pl.when(late & (l != m))
             def _():
@@ -438,17 +458,26 @@
                 def _():
                     hand_in(l, 0).start()
 
-            forward(l, l, True)
+            forward(l, l, l, l + 1)
+
+            @pl.when(early & (l == LAYERS - 1))
+            def _():
+                for c in range(CHUNKS):
+                    hop_f(c).start()
 
     @pl.when(busy & late)
     def _():
         decode()
+
+    @pl.when(guest)
+    def _():
+        guest_rows(0).wait_recv()
 
     @pl.when(busy)
     def _():
         @pl.loop(0, LAYERS)
         def _(l):
-            @pl.when((l != m) & (early | (l == 0)))
+            @pl.when((l != m) & (early | (l == 0)) & jnp.logical_not(guest & (l == 0)))
             def _():
                 hand_in(l, 0).start()
 
@@ -466,10 +495,15 @@
         other = jnp.where(early, t, t - LAYERS)
         l = LAYERS - 1 - jnp.where(early, t - samples, t)
 
-        @pl.when((other >= 0) & (other < samples) & (other != j))
-        def _():
-            handed_in(other, 0).wait_recv()
-            forward(LAYERS + other, m, False)
+        again = guest & (other == j)
+
+        @pl.when((other >= 0) & (other < samples) & ((other != j) | again) & jnp.logical_not(host & (other == GUEST)))
+        def _():
+            @pl.when(jnp.logical_not(again))
+            def _():
+                handed_in(other, 0).wait_recv()
+
+            forward(jnp.where(again, 1, LAYERS + other), jnp.where(again, 1, m), jnp.where(again, 1, LAYERS + 1 + other))
 
         @pl.when(busy & (l >= 0) & (l < LAYERS))
         def _():
@@ -526,8 +560,16 @@
             def _(l):
                 @pl.when(l != m)
                 def _():
-                    for kind in range(2):
-                        hand_in(l, kind).wait_send()
+                    @pl.when(jnp.logical_not(guest & (l == 0)))
+                    def _():
+                        hand_in(l, 0).wait_send()
+
+                    hand_in(l, 1).wait_send()
+
+        @pl.when(host)
+        def _():
+            for n in range(2):
+                guest_rows(n).wait_send()
 
     if not SUM:
         finish_sends()
@@ -698,7 +740,7 @@
         in_specs=[pl.BlockSpec(memory_space=pltpu.HBM)] * 12,
         out_specs=(vmem_spec, vmem_spec),
         scratch_shapes=[
-            v((grid_rows, features), BF16),
+            v((2, grid_rows, features), BF16),
             v((grid_rows, features), BF16),
             v((4,) + tile, BF16),
             v((4,) + tile, BF16),
@@ -714,14 +756,14 @@
             v((NODES, 2 * grid_rows), BF16),
             v((grid_rows, 2 * NODES), BF16),
             v((NODES, 2 * grid_rows), BF16),
+            v((LAYERS + 3 + samples, NODES, features), BF16),
+            v((LAYERS + 1 + samples, NODES, features), BF16),
             v((LAYERS + 1 + samples, NODES, features), BF16),
             v((LAYERS + 1 + samples, NODES, features), BF16),
             v((LAYERS + samples, NODES, features), BF16),
-            v((LAYERS + samples, NODES, features), BF16),
-            v((LAYERS + samples, NODES, features), BF16),
-            v((LAYERS + samples, NODES, features), F32),
-            v((LAYERS + samples, NODES, features), F32),
-            v((LAYERS, NODES, 128), F32),
+            v((LAYERS + 1 + samples, NODES, features), F32),
+            v((LAYERS + 1 + samples, NODES, features), F32),
+            v((LAYERS + 1 + samples, NODES, 128), F32),
             v((NODES, features), BF16),
             v((NODES, features), F32),
             v((LAYERS + samples, NODES, features), BF16),
@@ -734,7 +776,7 @@
             v((8, features), F32),
             v((RING, 8, features), F32),
             dma((10,)),
-            dma((2,)),
+            dma((3,)),
             dma((3, 3)),
             dma((3, 3)),
             dma((3, 3)),
@@ -743,6 +785,8 @@
             dma((3,)),
             dma((2, CHUNKS)),
             dma((2, CHUNKS)),
+            dma((2,)),
+            dma((2,)),
             dma((LAYERS, 2)),
             dma((samples, 2)),
             dma((RING,)),

time: 131 us -> 129 us (0.985); the launches traced: 131 us -> 127 us
  Pallas kernels: 128 us -> 125 us
    pallas_call x1, Pallas kernels: 128 us -> 125 us  [on_device(): pl.pallas_call(functools.partial(step_kernel, samples, loss_scale), out_s...]
where the time goes in v5:
time: 129 us; the launch traced here: 127 us
  Pallas kernels  125 us (97%)
  local copies, waits for them, and re-layouts  2.24 us (2%)
    pallas_call x1, Pallas kernels, on_device(): pl.pallas_call(functools.partial(step_kernel, samples, loss_scale), out_s...  125 us

profile of v5, /device:TPU:1, one launch (start us, length us, event | category | flops | bytes accessed | tf_op | source)
XLA Modules:
  0.0 127.5 jit_solution(2853620781490894919)
XLA Ops:
  0.6 124.6 %train_step.1 = (f32[1536,512]{1,0:T(8,128)S(1)}, f32[1,512]{1,0:T(1,128)S(1)}) custom-call(bf16[3,512,512]{2,1,0:T(8,128)(2,1)} %lat_hbm.1, bf16[3,512,512]{2,1,0:T(8,128)(2,1)} %tgt_hbm.1, bf16[4,128,128]{2,1,0:T(8,128)(2,1)} %g2m_hbm.1, s32[4]{0:T(128)} %g2m_c_hbm.1, bf16[4,128,128]{2,1,0:T(8,128)(2,1)} %m2m_hbm.1, s32[4]{0:T(128)} %m2m_c_hbm.1, ...), custom_call_target="tpu_custom_call" | custom-call | tf_op jit(solution)/shard_map/train_step/pallas_call | solution.py:734
  125.2 1.7 %copy.16 = f32[1,3,512,512]{3,2,1,0:T(8,128)} copy(f32[1,3,512,512]{3,2,1,0:T(8,128)S(1)} %bitcast.1) | data formatting | bytes 6291456
  126.9 0.6 copy.17

commit v6 on v5

--- a/solution.py
+++ b/solution.py
@@ -22,6 +22,7 @@
 STEPS = RING - 1
 FAR = RING // 2
 STREAMS = 4
+WIDE = 2
 SUM = True
 
 
@@ -82,6 +83,7 @@
     sib_buf,
     ring_buf,
     y_buf,
+    narrow,
     g_sib,
     g_y,
     g_z,
@@ -346,17 +348,22 @@
                 upstream = upstream + dot(part, residual)
         up[LAYERS] = upstream.astype(BF16)
 
+    def grad_unit(q, layer):
+        up_s[...] = dot_nt(gb_s[q], w[1, layer]) + dot_nt(gm_s[q], w[0, layer])
+
+    def add_gain_grads(q):
+        gacc[...] += jnp.sum((up_s[...] * normed_s[q]).reshape(NODES // 8, 8, features), axis=0)
+
     def backward(q, layer, own):
         gain = gains[layer, 0:1, :]
         gb_s[q] = (dot_nt(up[q + 1], w[2, layer]) * slope_s[q]).astype(BF16)
         gm_s[q] = (dot(mix_t[:, :NODES], gb_s[q]) + dot(mix_t[:, NODES:], gb_s[q])).astype(BF16)
-        up_s[...] = dot_nt(gb_s[q], w[1, layer]) + dot_nt(gm_s[q], w[0, layer])
-
-        @pl.when(layer == m)
-        def _():
-            gacc[...] += jnp.sum((up_s[...] * normed_s[q]).reshape(NODES // 8, 8, features), axis=0)
-
         if own:
+            grad_unit(q, layer)
+
+            @pl.when(layer == m)
+            def _():
+                add_gain_grads(q)
 
             @pl.when(late | (q > 0))
             def _():
@@ -571,7 +578,16 @@
             for n in range(2):
                 guest_rows(n).wait_send()
 
+    def other_gain_grads():
+        @pl.loop(0, samples)
+        def _(i):
+            @pl.when(i != j)
+            def _():
+                grad_unit(LAYERS + i, m)
+                add_gain_grads(LAYERS + i)
+
     if not SUM:
+        other_gain_grads()
         finish_sends()
         return
 
@@ -609,7 +625,6 @@
     g_to_sib = remote(gacc, g_sib, gs_sem.at[0], gs_sem.at[1], sibling)
     for shift in (4, 3, 5, 2, 6, 1, 7, 0):
         to_sib(shift).start()
-    g_to_sib.start()
 
     def rs(u, d, t):
         rows = rows_at(core, u, owner_at(d, steps(u, d) - t))
@@ -635,11 +650,14 @@
     from_sib(1, 7)
     start_pair(3)
     from_sib(0)
-    g_to_sib.wait()
-    gacc[...] += g_sib[...]
+    other_gain_grads()
+    g_to_sib.start()
     g_to_y = remote(gacc, g_y, gy_sem.at[0], gy_sem.at[1], across)
-    g_to_y.start()
     for t in range(1, FAR):
+        if t == 2:
+            g_to_sib.wait()
+            gacc[...] += g_sib[...]
+            g_to_y.start()
         for u, d in flows:
             if t < steps(u, d):
                 take(u, d, t - 1)
@@ -666,29 +684,41 @@
     for d in range(1, RING):
         g_spread(d).start()
 
+    def finished(c, u, owner):
+        return out.at[rows_at(c, u, owner)] if u < WIDE else narrow.at[c, u - WIDE, owner]
+
+    def widen(c, u, owner):
+        if u >= WIDE:
+            out[rows_at(c, u, owner), :] = narrow[c, u - WIDE, owner].astype(F32)
+
     def spread(u, d, t):
-        rows = rows_at(core, u, owner_at(1 - d, t))
-        return remote(out.at[rows], out.at[rows], ag_send.at[u, d, t], ag_recv.at[u, d, t], toward(d))
+        here = finished(core, u, owner_at(1 - d, t))
+        return remote(here, here, ag_send.at[u, d, t], ag_recv.at[u, d, t], toward(d))
 
     def arrive(u, d, t):
-        rows = rows_at(core, u, owner_at(1 - d, t + 1))
-        return remote(out.at[rows], out.at[rows], ag_send.at[u, d, t], ag_recv.at[u, d, t], toward(d))
+        here = finished(core, u, owner_at(1 - d, t + 1))
+        return remote(here, here, ag_send.at[u, d, t], ag_recv.at[u, d, t], toward(d))
 
     def hand_over(u, owner):
-        rows = rows_at(core, u, owner)
-        return remote(out.at[rows], out.at[rows], fw_send.at[u, owner], fw_recv.at[u, owner], sibling)
+        here = finished(core, u, owner)
+        return remote(here, here, fw_send.at[u, owner], fw_recv.at[u, owner], sibling)
 
     def handed_over(u, owner):
-        rows = rows_at(1 - core, u, owner)
-        return remote(out.at[rows], out.at[rows], fw_send.at[u, owner], fw_recv.at[u, owner], sibling)
+        here = finished(1 - core, u, owner)
+        return remote(here, here, fw_send.at[u, owner], fw_recv.at[u, owner], sibling)
 
     for u in range(STREAMS):
         y_copy(u).wait()
         rows = rows_at(core, u, z)
-        out[rows, :] = acc[rows, :] + y_buf[u]
+        total = acc[rows, :] + y_buf[u]
+        if u < WIDE:
+            out[rows, :] = total
+        else:
+            narrow[core, u - WIDE, z] = total.astype(BF16)
         for d in (u % 2, 1 - u % 2):
             spread(u, d, 0).start()
         hand_over(u, z).start()
+        widen(core, u, z)
 
     for t in range(FAR):
         for u, d in flows:
@@ -697,6 +727,7 @@
                 if t + 1 < steps(u, d):
                     spread(u, d, t + 1).start()
                 hand_over(u, owner_at(1 - d, t + 1)).start()
+                widen(core, u, owner_at(1 - d, t + 1))
 
     for d in range(1, RING):
         g_arrive(d).wait_recv()
@@ -710,6 +741,7 @@
     for u in range(STREAMS):
         for i in range(RING):
             handed_over(u, i).wait_recv()
+            widen(1 - core, u, i)
             hand_over(u, i).wait_send()
     for u, d in flows:
         for t in range(steps(u, d)):
@@ -772,6 +804,7 @@
             v((RING, chunk, features), F32),
             v((STREAMS, 2, FAR, piece, features), F32),
             v((STREAMS, piece, features), F32),
+            v((CORES, STREAMS - WIDE, RING, piece, features), BF16),
             v((8, features), F32),
             v((8, features), F32),
             v((RING, 8, features), F32),

time: 129 us -> 127 us (0.984)
  Pallas kernels: 125 us -> 123 us
    pallas_call x1, Pallas kernels: 125 us -> 123 us  [on_device(): pl.pallas_call(functools.partial(step_kernel, samples, loss_scale), out_s...]
where the time goes in v6:
time: 127 us; the launch traced here: 126 us
  Pallas kernels  123 us (97%)
  local copies, waits for them, and re-layouts  2.24 us (2%)
    pallas_call x1, Pallas kernels, on_device(): pl.pallas_call(functools.partial(step_kernel, samples, loss_scale), out_s...  123 us

profile of v6, /device:TPU:1, one launch (start us, length us, event | category | flops | bytes accessed | tf_op | source)
XLA Modules:
  0.0 126.0 jit_solution(5698212479915430827)
XLA Ops:
  0.6 123.1 %train_step.1 = (f32[1536,512]{1,0:T(8,128)S(1)}, f32[1,512]{1,0:T(1,128)S(1)}) custom-call(bf16[3,512,512]{2,1,0:T(8,128)(2,1)} %lat_hbm.1, bf16[3,512,512]{2,1,0:T(8,128)(2,1)} %tgt_hbm.1, bf16[4,128,128]{2,1,0:T(8,128)(2,1)} %g2m_hbm.1, s32[4]{0:T(128)} %g2m_c_hbm.1, bf16[4,128,128]{2,1,0:T(8,128)(2,1)} %m2m_hbm.1, s32[4]{0:T(128)} %m2m_c_hbm.1, ...), custom_call_target="tpu_custom_call" | custom-call | tf_op jit(solution)/shard_map/train_step/pallas_call | solution.py:766
  123.7 1.7 %copy.16 = f32[1,3,512,512]{3,2,1,0:T(8,128)} copy(f32[1,3,512,512]{3,2,1,0:T(8,128)S(1)} %bitcast.1) | data formatting | bytes 6291456
  125.4 0.6 copy.17

commit v7 on v6

--- a/solution.py
+++ b/solution.py
@@ -19,7 +19,6 @@
 LAYERS = 4
 CORES = 2
 RING = 8
-STEPS = RING - 1
 FAR = RING // 2
 STREAMS = 4
 WIDE = 2
@@ -169,9 +168,9 @@
     met = 5
     if SUM:
         greet(across)
-        for d in range(1, RING):
-            greet(dp_at(yh, lax.rem(z + d, RING), core))
-        met += RING
+        greet(dp_at(yh, z_next, core))
+        greet(dp_at(yh, z_prev, core))
+        met += 3
 
     w_hbm = (wm_hbm, wu_hbm, wd_hbm)
     loads = [
@@ -674,15 +673,16 @@
     g_to_y.wait()
     g_z[z] = gacc[...] + g_y[...]
 
-    def g_spread(d):
-        return remote(g_z.at[z], g_z.at[z], gz_send.at[d - 1], gz_recv.at[d - 1], dp_at(yh, lax.rem(z + d, RING), core))
-
-    def g_arrive(d):
-        at = lax.rem(z - d + RING, RING)
-        return remote(g_z.at[at], g_z.at[at], gz_send.at[d - 1], gz_recv.at[d - 1], dp_at(yh, at, core))
-
-    for d in range(1, RING):
-        g_spread(d).start()
+    def g_pass(d, t):
+        here = g_z.at[owner_at(1 - d, t)]
+        return remote(here, here, gz_send.at[d, t], gz_recv.at[d, t], toward(d))
+
+    def g_arrive(d, t):
+        here = g_z.at[owner_at(1 - d, t + 1)]
+        return remote(here, here, gz_send.at[d, t], gz_recv.at[d, t], toward(d))
+
+    for d in range(2):
+        g_pass(d, 0).start()
 
     def finished(c, u, owner):
         return out.at[rows_at(c, u, owner)] if u < WIDE else narrow.at[c, u - WIDE, owner]
@@ -728,9 +728,11 @@
                     spread(u, d, t + 1).start()
                 hand_over(u, owner_at(1 - d, t + 1)).start()
                 widen(core, u, owner_at(1 - d, t + 1))
-
-    for d in range(1, RING):
-        g_arrive(d).wait_recv()
+                if u == d and t < FAR - d:
+                    g_arrive(d, t).wait_recv()
+                    if t + 1 < FAR - d:
+                        g_pass(d, t + 1).start()
+
     total = g_z[0]
     for i in range(1, RING):
         total = total + g_z[i]
@@ -748,8 +750,9 @@
             if t > 0 or (u, d) in pairs[-1]:
                 rs(u, d, t).wait_send()
             spread(u, d, t).wait_send()
-    for d in range(1, RING):
-        g_spread(d).wait_send()
+    for d in range(2):
+        for t in range(FAR - d):
+            g_pass(d, t).wait_send()
     finish_sends()
 
 
@@ -834,8 +837,8 @@
             dma((STREAMS, RING)),
             dma((2,)),
             dma((2,)),
-            dma((STEPS,)),
-            dma((STEPS,)),
+            dma((2, FAR)),
+            dma((2, FAR)),
         ],
         compiler_params=pltpu.CompilerParams(
             collective_id=0, has_side_effects=True, vmem_limit_bytes=44 * 1024 * 1024

time: 127 us -> 127 us (level)
  no operation moved by 1% of the time
where the time goes in v7:
time: 127 us; the launch traced here: 125 us
  Pallas kernels  123 us (97%)
  local copies, waits for them, and re-layouts  2.24 us (2%)
    pallas_call x1, Pallas kernels, on_device(): pl.pallas_call(functools.partial(step_kernel, samples, loss_scale), out_s...  123 us

profile of v7, /device:TPU:1, one launch (start us, length us, event | category | flops | bytes accessed | tf_op | source)
XLA Modules:
  0.0 125.4 jit_solution(12934843681403484485)
XLA Ops:
  0.6 122.5 %train_step.1 = (f32[1536,512]{1,0:T(8,128)S(1)}, f32[1,512]{1,0:T(1,128)S(1)}) custom-call(bf16[3,512,512]{2,1,0:T(8,128)(2,1)} %lat_hbm.1, bf16[3,512,512]{2,1,0:T(8,128)(2,1)} %tgt_hbm.1, bf16[4,128,128]{2,1,0:T(8,128)(2,1)} %g2m_hbm.1, s32[4]{0:T(128)} %g2m_c_hbm.1, bf16[4,128,128]{2,1,0:T(8,128)(2,1)} %m2m_hbm.1, s32[4]{0:T(128)} %m2m_c_hbm.1, ...), custom_call_target="tpu_custom_call" | custom-call | tf_op jit(solution)/shard_map/train_step/pallas_call | solution.py:769
  123.1 1.7 %copy.16 = f32[1,3,512,512]{3,2,1,0:T(8,128)} copy(f32[1,3,512,512]{3,2,1,0:T(8,128)S(1)} %bitcast.1) | data formatting | bytes 6291456
  124.8 0.6 copy.17

commit v8 on v7

--- a/solution.py
+++ b/solution.py
@@ -279,6 +279,7 @@
     give(1, 2).start()
     give(2, 0).wait_send()
     give(2, 1).start()
+    give(2, 2).start()
 
     span = NODES // CHUNKS
 
@@ -408,8 +409,6 @@
                 if k == 2:
                     give(3, i).start()
                 share(k, i).start()
-            give(2, 1).wait_send()
-            give(2, 2).start()
             for i in range(3):
                 shared(1, i).wait_recv()
 
@@ -532,7 +531,7 @@
 
     @pl.loop(0, samples)
     def _(t):
-        i = lax.rem(j + t, samples)
+        i = lax.rem(j + jnp.where(host, samples - t, t), samples)
         mine = i == j
 
         @pl.when(jnp.logical_not(mine))
@@ -546,7 +545,7 @@
         for k in (1, 2, 3):
             give_gain(k).wait_send()
             for i in range(3):
-                if (k, i) not in ((1, 0), (2, 0), (2, 1)):
+                if (k, i) not in ((1, 0), (2, 0)):
                     give(k, i).wait_send()
                 share(k, i).wait_send()
 

time: 127 us -> 126 us (level)
  Pallas kernels: 123 us -> 121 us
    pallas_call x1, Pallas kernels: 123 us -> 121 us  [on_device(): pl.pallas_call(functools.partial(step_kernel, samples, loss_scale), out_s...]
where the time goes in v8:
time: 126 us; the launch traced here: 124 us
  Pallas kernels  121 us (96%)
  local copies, waits for them, and re-layouts  2.24 us (2%)
    pallas_call x1, Pallas kernels, on_device(): pl.pallas_call(functools.partial(step_kernel, samples, loss_scale), out_s...  121 us

profile of v8, /device:TPU:1, one launch (start us, length us, event | category | flops | bytes accessed | tf_op | source)
XLA Modules:
  0.0 124.1 jit_solution(11759419220673754846)
XLA Ops:
  0.6 121.2 %train_step.1 = (f32[1536,512]{1,0:T(8,128)S(1)}, f32[1,512]{1,0:T(1,128)S(1)}) custom-call(bf16[3,512,512]{2,1,0:T(8,128)(2,1)} %lat_hbm.1, bf16[3,512,512]{2,1,0:T(8,128)(2,1)} %tgt_hbm.1, bf16[4,128,128]{2,1,0:T(8,128)(2,1)} %g2m_hbm.1, s32[4]{0:T(128)} %g2m_c_hbm.1, bf16[4,128,128]{2,1,0:T(8,128)(2,1)} %m2m_hbm.1, s32[4]{0:T(128)} %m2m_c_hbm.1, ...), custom_call_target="tpu_custom_call" | custom-call | tf_op jit(solution)/shard_map/train_step/pallas_call | solution.py:768
  121.8 1.7 %copy.16 = f32[1,3,512,512]{3,2,1,0:T(8,128)} copy(f32[1,3,512,512]{3,2,1,0:T(8,128)S(1)} %bitcast.1) | data formatting | bytes 6291456
  123.5 0.6 copy.17
